TPU v7x, 32 devices: a whole 2x2x4 slice. The times are simulated.
32 devices in a mesh: dp: 8 (over z, x), segment: 4 (over y, core).
Axes of the slice: x: 2, y: 2, z: 4, core: 2. Of those that a mesh axis runs over, the one named last changes fastest.
Arguments:
- latents: float32 [24, 4, 4, 16, 16], P('dp'), may hold values from -6 to 6
- noise_draw: float32 [24, 4, 4, 16, 16], P('dp'), may hold values from -6 to 6
- timesteps: int32 [24], P('dp'), may hold values from 1 to 999
- captions: bfloat16 [24, 300, 4096], P('dp'), may hold values from -2 to 2
- caption_len: int32 [24], P('dp'), may hold values from 1 to 300, as said below
- attention_weights: float32 [12, 384, 384], P(None, None, 'dp'), may hold values from -0.3125 to 0.3125
- feed_weights: float32 [4, 384, 1536], P(None, None, 'dp')
- side_weights: float32 [7456, 384], P(None, 'dp')
- vector_weights: float32 [45, 384], P(None, 'dp'), may hold values from -3 to 3
- attention_momentum: float32 [12, 384, 384], P(None, None, 'dp'), may hold values from -2.670288e-05 to 2.670288e-05
- feed_momentum: float32 [4, 384, 1536], P(None, None, 'dp'), may hold values from -2.670288e-05 to 2.670288e-05
- side_first: float32 [7456, 384], P(None, 'dp'), may hold values from -3.33786e-06 to 3.33786e-06
- side_second: float32 [7456, 384], P(None, 'dp'), may hold values from 3.566765e-15 to 1.426706e-14
- vector_first: float32 [45, 384], P(None, 'dp'), may hold values from -3.0517578e-05 to 3.0517578e-05
- vector_second: float32 [45, 384], P(None, 'dp'), may hold values from 3.5667652e-13 to 1.4267061e-12
- step_count: int32 [1], replicated, may hold values from 2 to 20
Outputs:
- loss_value: float32 [], replicated
- grad_norm: float32 [], replicated
- attention_new: float32 [12, 384, 384], P(None, None, 'dp')
- attention_moment: float32 [12, 384, 384], P(None, None, 'dp')
- feed_new: float32 [4, 384, 1536], P(None, None, 'dp')
- feed_moment: float32 [4, 384, 1536], P(None, None, 'dp')
- side_new: float32 [7456, 384], P(None, 'dp')
- side_first_new: float32 [7456, 384], P(None, 'dp')
- side_second_new: float32 [7456, 384], P(None, 'dp')
- vector_new: float32 [45, 384], P(None, 'dp')
- vector_first_new: float32 [45, 384], P(None, 'dp')
- vector_second_new: float32 [45, 384], P(None, 'dp')
- attention_bf16: bfloat16 [12, 384, 384], P(None, None, 'dp')
- feed_bf16: bfloat16 [4, 384, 1536], P(None, None, 'dp')
- side_bf16: bfloat16 [7456, 384], P(None, 'dp')
- vector_bf16: bfloat16 [45, 384], P(None, 'dp')
Inputs may be any that keep to these rules, and one draw needn't show every extreme that they name: `caption_len`: each clip has 1 to 300 valid caption tokens, the first clip exactly 300.
All inputs are finite; a program needn't handle non-finite values.
Results may differ from a plain program's by a relative error of at most 0.0015.
The roundings to bfloat16 on the way count: a program that leaves them out, or rounds other values in their place, can miss the bound.
Values may be sent and summed in bfloat16 or wider, within the bound.
A program may use at most 256 MiB of HBM per device.

v0:
```python
import functools
import math

import jax
import jax.numpy as jnp
import numpy as np
from jax import lax
from jax.experimental import pallas as pl
from jax.experimental.pallas import tpu as pltpu
from jax.sharding import PartitionSpec as P

HEADS = 6
HEAD = 64
LP = 304
KP = 384

highest = lax.Precision.HIGHEST
snr_gamma = 5.0
max_norm = 0.005
momentum_decay = 0.95
muon_rate = 0.05
adam_rate = 0.02
beta_one = 0.9
beta_two = 0.999
weight_decay = 0.01
coef_a = 3.4445
coef_b = -4.775
coef_c = 2.0315

f32, bf16 = jnp.float32, jnp.bfloat16
MESH = pl.DeviceIdType.MESH
ANY = pl.BlockSpec(memory_space=pl.ANY)
VM = pl.BlockSpec(memory_space=pltpu.VMEM)
SM = pl.BlockSpec(memory_space=pltpu.SMEM)
VMEM_LIMIT = 60000 * 1024


def low(value):
    return value.astype(bf16)


def nt(left, right):
    return lax.dot_general(left, right, (((1,), (1,)), ((), ())), preferred_element_type=f32)


def nn(left, right):
    return lax.dot_general(left, right, (((1,), (0,)), ((), ())), preferred_element_type=f32)


def tn(left, right):
    return lax.dot_general(left, right, (((0,), (0,)), ((), ())), preferred_element_type=f32)


def snr_weight(steps_t):
    level = jnp.cos((steps_t / 1000.0 + 0.008) / 1.008 * (math.pi / 2)) ** 2
    ratio = level / (1.0 - level)
    return level, jnp.minimum(ratio, snr_gamma) / ratio


def patchify(frames):
    clips, count, channels, height, breadth = frames.shape
    grid = frames.reshape(clips, count, channels, height // 2, 2, breadth // 2, 2)
    grid = grid.transpose(0, 1, 3, 5, 4, 6, 2)
    return grid.reshape(clips, count, (height // 2) * (breadth // 2), 4 * channels)


def sincos(places, model_width):
    half_width = model_width // 2
    freqs = np.exp(-math.log(10000.0) * np.arange(half_width) / half_width)
    angles = places[:, None] * freqs[None, :]
    return np.concatenate([np.sin(angles), np.cos(angles)], axis=1).astype(np.float32)


def col_sum(value):
    return jnp.sum(value.astype(f32), axis=0, keepdims=True)


def norm(value):
    centred = value - jnp.mean(value, axis=-1, keepdims=True)
    inv = lax.rsqrt(jnp.mean(centred * centred, axis=-1, keepdims=True) + 1e-06)
    return centred * inv, inv


def norm_back(grad, normed, inv):
    return inv * (
        grad
        - jnp.mean(grad, axis=-1, keepdims=True)
        - normed * jnp.mean(grad * normed, axis=-1, keepdims=True)
    )


GELU_C = math.sqrt(2.0 / math.pi)


def gelu(value):
    inner = GELU_C * (value + 0.044715 * (value * value * value))
    return value * (0.5 * (1.0 + jnp.tanh(inner)))


def gelu_both(value):
    square = value * value
    tanh = jnp.tanh(GELU_C * (value + 0.044715 * (square * value)))
    cdf = 0.5 * (1.0 + tanh)
    slope = 0.5 * (1.0 - tanh * tanh) * (GELU_C * (1.0 + 3 * 0.044715 * square))
    return value * cdf, cdf + value * slope


def lanes_low():
    lane = lax.broadcasted_iota(jnp.int32, (1, 128), 1)
    first = jnp.where(lane < HEAD, 1.0, 0.0)
    return low(first), low(1.0 - first), lane < HEAD


def stack_heads(pair, first, second):
    return jnp.concatenate([pair * first, pair * second], axis=0)


def attend(queries, keys, values, allowed):
    first, second, lower = lanes_low()
    rows = queries.shape[0]
    mixed, probs = [], []
    for pair in range(HEADS // 2):
        cut = slice(pair * 128, pair * 128 + 128)
        scores = nt(stack_heads(queries[:, cut], first, second), keys[:, cut]) * 0.125
        scores = jnp.where(allowed, scores, -1e30)
        weight = jnp.exp(scores - jnp.max(scores, axis=-1, keepdims=True))
        prob = weight / jnp.sum(weight, axis=-1, keepdims=True)
        probs.append(prob)
        out = nn(low(prob), values[:, cut])
        mixed.append(jnp.where(lower, out[:rows], out[rows:]))
    return low(jnp.concatenate(mixed, axis=1)), probs


def attend_back(grad, queries, keys, values, probs):
    first, second, lower = lanes_low()
    rows = queries.shape[0]
    dq, dk, dv = [], [], []
    for pair in range(HEADS // 2):
        cut = slice(pair * 128, pair * 128 + 128)
        stacked = stack_heads(grad[:, cut], first, second)
        prob = probs[pair]
        dv.append(tn(low(prob), stacked))
        dprob = nt(stacked, values[:, cut])
        dscore = low(prob * (dprob - jnp.sum(prob * dprob, axis=-1, keepdims=True)))
        part = nn(dscore, keys[:, cut])
        dq.append(jnp.where(lower, part[:rows], part[rows:]) * 0.125)
        dk.append(tn(dscore, stack_heads(queries[:, cut], first, second)) * 0.125)
    return tuple(jnp.concatenate(piece, axis=1) for piece in (dq, dk, dv))


def self_forward(x, mods, weights, bias, allowed):
    normed, inv = norm(x)
    a = low(normed * (1.0 + mods[1]) + mods[0])
    q = low(nt(a, weights[0]) + bias[0])
    k = low(nt(a, weights[1]))
    v = low(nt(a, weights[2]) + bias[1])
    o, probs = attend(q, k, v, allowed)
    branch = nt(o, weights[3]) + bias[2]
    return x + mods[2] * branch, (normed, inv, a, q, k, v, o, probs, branch)


def self_backward(dx, kept, mods, weights):
    normed, inv, a, q, k, v, o, probs, branch = kept
    dm2 = col_sum(dx * branch)
    dbr = low(dx * mods[2])
    do = low(nn(dbr, weights[3]))
    dq, dk, dv = (low(piece) for piece in attend_back(do, q, k, v, probs))
    da = nn(dq, weights[0]) + nn(dk, weights[1]) + nn(dv, weights[2])
    dm1, dm0 = col_sum(da * normed), col_sum(da)
    dx = dx + norm_back(da * (1.0 + mods[1]), normed, inv)
    return dx, (dm0, dm1, dm2), (col_sum(dq), col_sum(dv), col_sum(dbr)), (a, dq, dk, dv, o, dbr)


def feed_forward(x, mods, feed, bias_up, bias_down):
    normed, inv = norm(x)
    c = low(normed * (1.0 + mods[4]) + mods[3])
    u = nt(c, feed[0]) + bias_up
    g = low(gelu(u))
    branch = nn(g, feed[1]) + bias_down
    return x + mods[5] * branch, (normed, inv, c, u, g, branch)


def feed_backward(dx, kept, mods, feed):
    normed, inv, c, u, g, branch = kept
    dm5 = col_sum(dx * branch)
    dbr = low(dx * mods[5])
    value, slope = gelu_both(u)
    g = low(value)
    du = low(nt(dbr, feed[1]) * slope)
    dc = nn(du, feed[0])
    dm4, dm3 = col_sum(dc * normed), col_sum(dc)
    dx = dx + norm_back(dc * (1.0 + mods[4]), normed, inv)
    return dx, (dm3, dm4, dm5), (col_sum(du), col_sum(dbr)), (c, dbr, du, g)


def pair_mask(kind):
    row = lax.broadcasted_iota(jnp.int32, (256, 128), 0) % 128
    col = lax.broadcasted_iota(jnp.int32, (256, 128), 1)
    if kind == 0:
        return row // 64 == col // 64
    return row % 32 == col % 32


VEC0, EMB0, HEAD0 = 0, 45, 61


def mod_rows(mq, vec, table, clip):
    rows = []
    for r in range(6):
        at = (r % 3) * 384
        rows.append(
            mq[r // 3, pl.ds(clip, 1), at : at + 384]
            + vec[3 + r : 4 + r]
            + vec[table + r : table + r + 1]
        )
    return rows


def up_bias(vec, start):
    return jnp.concatenate([vec[start + i : start + i + 1] for i in range(4)], axis=1)


def pack_kernel(role, half, offsets, att, feed, side, vec, pa, pb, pf, pw, py, pm, wm):
    time, text, text2, head, mod = offsets
    width, per, rows = att.shape[2], pf.shape[0], py.shape[0]

    def rounded(at, size):
        return low(side[:, at : at + size])

    first = text - time
    pw[:, 0:first] = rounded(time, first)
    pw[:, first : first + width] = rounded(text2, width)
    cols = pw.shape[0]
    pw[:, first + width :] = low(jnp.concatenate(
        [vec[...], side[:, 0:16], side[:, head : head + 16], jnp.zeros((cols, 51), f32)], axis=1
    ))
    wm[...] = rounded(mod, 6 * width)
    for r in range(2):

        @pl.when(role[0] == r)
        def _():
            pa[...] = low(att[4 * r : 4 * r + 4])
            pf[...] = low(feed[per * r : per * r + per])
            if r == 1:
                pb[...] = low(att[8:12])

    for h in range(2):

        @pl.when(half[0] == h)
        def _():
            pm[...] = rounded(mod + h * 3 * width, 3 * width)
            top = min((h + 1) * rows, cols)
            py[0 : top - h * rows, :] = low(side[h * rows : top, text : text + py.shape[1]])


def units_of(hand, lanes, width, cols):
    per = -(-cols // 2)
    unit = lax.broadcasted_iota(jnp.int32, (lanes, width), 0)
    column = lax.broadcasted_iota(jnp.int32, (lanes, width), 1)
    inside = hand * per + unit % per
    match = jnp.logical_and((unit // per) * cols + inside == column, inside < cols)
    return low(jnp.where(match, 1.0, 0.0))


def condition_kernel(rank, wt, ww, wm, vec, hid, temb, mq, y2p, errs, *, per_clip, cols):
    turned = jnp.transpose(ww[:, 1024:1152].astype(f32))
    vec[...] = turned
    feature = low(wt[:, 0:256])
    first = nt(feature, ww[:, 0:256]) + turned[1:2]
    hid[...] = first
    second = nt(low(first * jax.nn.sigmoid(first)), ww[:, 256:640]) + turned[2:3]
    temb[...] = second
    own = temb[pl.ds(pl.multiple_of(rank[0] * 8, 8), 8), :]
    mq[...] = nn(low(own * jax.nn.sigmoid(own)), wm[...])
    for h in range(2):
        y2p[h] = low(nt(ww[:, 640:1024], units_of(h, y2p.shape[2], y2p.shape[1], cols)))
    total = jnp.sum(wt[:, 256:257], axis=0, keepdims=True)
    weight = wt[pl.ds(pl.multiple_of(rank[0] * 8, 8), 8), 256:257] / (total * (per_clip * 16.0))
    errs[...] = jnp.broadcast_to(weight, errs.shape)


def embed_chunk(tok_ref, vec, pos_ref, chunk):
    tokens = tok_ref[pl.ds(pl.multiple_of(chunk * 128, 128), 128), :]
    places = pos_ref[...] + vec[0:1]
    return low(nn(tokens, low(vec[...])) + jnp.concatenate([places, places], axis=0)), tokens


def spatial_bias(vec):
    return (vec[11:12], vec[12:13], vec[13:14])


def residual_copies(sources, targets, sems):
    def of(chunk):
        rows = pl.ds(pl.multiple_of(chunk * 128, 128), 128)
        cuts = [lambda r: r.at[:, rows], lambda r: r.at[:, rows], lambda r: r.at[rows],
                lambda r: r.at[chunk]]
        return [
            pltpu.make_async_copy(cut(src), cut(dst), sems.at[chunk, i])
            for i, (cut, src, dst) in enumerate(zip(cuts, sources, targets))
        ]

    return of


def first_kernel(
    cols, role, half, tok, pos, mq, vec, wa, wf, wy, captions,
    h1, hq, gq, out_b, out_f, out_u, out_p, kept_b, kept_f, kept_u, kept_p, cap, sems, ksem,
):
    @pl.when(role[0] == 1)
    def _():
        clips = captions.shape[0]
        for c in range(clips):
            pltpu.make_async_copy(captions.at[c], cap.at[c], sems.at[c]).start()
        bias = nt(low(vec[9:10]), units_of(half[0], wy.shape[0], vec.shape[1], cols))
        def layer(c, carry):
            pltpu.make_async_copy(captions.at[c], cap.at[c], sems.at[c]).wait()
            value = nt(cap[c], wy[...]) + bias
            rows = value.shape[0]
            pad = jnp.zeros((LP - rows, value.shape[1]), f32)
            hq[c] = jnp.concatenate([value, pad], axis=0)
            gq[c] = low(jnp.concatenate([gelu(value), pad], axis=0))
            return carry

        lax.fori_loop(0, clips, layer, 0)

    @pl.when(role[0] == 0)
    def _():
        allowed = pair_mask(0)
        count = h1.shape[0]
        bu = up_bias(vec, 14)
        residuals = residual_copies((kept_b, kept_f, kept_u, kept_p), (out_b, out_f, out_u, out_p), ksem)

        def step(chunk, carry):
            @pl.when(chunk > 0)
            def _():
                for copy in residuals(chunk - 1):
                    copy.start()

            m = mod_rows(mq, vec, 19, (half[0] * count + chunk) // 2)
            h0, _ = embed_chunk(tok, vec, pos, chunk)
            x1, kept = self_forward(h0.astype(f32), m, wa, spatial_bias(vec), allowed)
            x, kept_feed = feed_forward(x1, m, wf, bu, vec[18:19])
            out = low(x)
            where = pl.ds(pl.multiple_of(chunk * 128, 128), 128)
            for i, value in enumerate((h0,) + kept[3:7]):
                kept_b[i, where, :] = value
            for i, value in enumerate((x1, kept[8], kept_feed[5])):
                kept_f[i, where, :] = value
            kept_u[where, :] = kept_feed[3]
            for pair in range(3):
                kept_p[chunk, pair] = kept[7][pair]
            for frame in range(2):
                for part in range(2):
                    start = frame * 64 + part * 32
                    h1[chunk, part, frame * 32 : frame * 32 + 32, :] = out[start : start + 32]
            return carry

        lax.fori_loop(0, count, step, 0)
        for copy in residuals(count - 1):
            copy.start()
        for chunk in range(count):
            for copy in residuals(chunk):
                copy.wait()


def last_kernel(
    role, half, tok, mq, vec, wa, wb, wf, in_b, in_f, in_u, in_p, dh, dkv, extra, grads_t, dmod_t,
    acts, actf, actw, dkvb, dy, vect, dmod, grads, kept_b, kept_f, kept_u, kept_p, ksem,
):
    @pl.when(role[0] == 0)
    def _():
        grads[...] = jnp.zeros_like(grads)
        dmod[...] = jnp.zeros_like(dmod)
        count = dh.shape[0]
        residuals = residual_copies((in_b, in_f, in_u, in_p), (kept_b, kept_f, kept_u, kept_p), ksem)
        for chunk in range(count):
            for copy in residuals(chunk):
                copy.start()

        def step(chunk, carry):
            for copy in residuals(chunk):
                copy.wait()
            m = mod_rows(mq, vec, 19, (half[0] * count + chunk) // 2)
            where = pl.ds(pl.multiple_of(chunk * 128, 128), 128)
            tokens = tok[where, :]
            h0, q, k, v, o = (kept_b[i, where, :] for i in range(5))
            x1, branch, branch_f = (kept_f[i, where, :] for i in range(3))
            normed, inv = norm(h0.astype(f32))
            a = low(normed * (1.0 + m[1]) + m[0])
            probs = [kept_p[chunk, pair] for pair in range(3)]
            kept = (normed, inv, a, q, k, v, o, probs, branch)
            normed_f, inv_f = norm(x1)
            c = low(normed_f * (1.0 + m[4]) + m[3])
            kept_feed = (normed_f, inv_f, c, kept_u[where, :], None, branch_f)
            parts = []
            for frame in range(2):
                for part in range(2):
                    parts.append(dh[chunk, part, frame * 32 : frame * 32 + 32, :])
            dx = jnp.concatenate(parts, axis=0).astype(f32)
            dx, dm_f, db_f, act_f = feed_backward(dx, kept_feed, m, wf)
            dx, dm_a, db_a, act_a = self_backward(dx, kept, m, wa)
            dh0 = low(dx)
            for i, value in enumerate(act_a):
                acts[i, where, :] = value
            for i in range(2):
                actf[i, where, :] = act_f[i]
                actw[i, where, :] = act_f[2 + i]
            mods = dm_a + dm_f
            dmod[chunk, 0:6, :] = jnp.concatenate(mods, axis=0)
            grads[...] += tn(tokens, dh0)
            grads[0:1] += col_sum(dh0)
            for i in range(3):
                grads[11 + i : 12 + i] += db_a[i]
            for i in range(4):
                grads[14 + i : 15 + i] += db_f[0][:, i * 384 : i * 384 + 384]
            grads[18:19] += db_f[1]
            for i in range(6):
                grads[19 + i : 20 + i] += mods[i]
            return carry

        lax.fori_loop(0, count, step, 0)

    @pl.when(role[0] == 1)
    def _():
        grads[...] = grads_t[...]
        dmod[...] = dmod_t[...]
        dy[...] = jnp.zeros_like(dy)
        dkvb[...] = jnp.zeros_like(dkvb)
        ncl = dy.shape[0]
        for c in range(ncl):

            @pl.when(jnp.logical_or(half[0] == 0, c > 0))
            def _():
                pieces = []
                for i in range(2):
                    value = dkv[i, c]
                    if c == ncl - 1:
                        value = value + jnp.where(half[0] == 0, extra[i], 0.0)
                    pieces.append(low(value))
                dkvb[0, c], dkvb[1, c] = pieces
                back = low(nn(pieces[0], wb[1]) + nn(pieces[1], wb[2]))
                dy[c] = back
                grads[40:41] += col_sum(pieces[1])
                grads[10:11] += col_sum(back)

    vect[...] = jnp.transpose(grads[...])


def temporal_kernel(
    role, half, rank, lens, errw, h1, timing, mq, vec, temb, wa, wb, wf, gq, rgq, y2p, target,
    dh1, acts, actf, actw, ybuf, dkv, grads, dmod, loss, kx, vx,
):
    @pl.when(role[0] == 0)
    def _():
        loss[...] = jnp.zeros_like(loss)

    @pl.when(role[0] == 1)
    def _():
        allowed = pair_mask(1)
        count = h1.shape[0]
        ncl = ybuf.shape[0]
        for ref in (kx, vx, dkv, grads, loss):
            ref[...] = jnp.zeros_like(ref)
        first_clip = (half[0] * count) // 2

        def features(c, carry):
            clip = jnp.minimum(first_clip + c, gq.shape[0] - 1)
            y = nt(gq[clip], y2p[half[0]]) + nt(rgq[clip], y2p[1 - half[0]])
            y = low(y + vec[10:11])
            ybuf[c] = y
            kx[c, 0:LP, :] = low(nt(y, wb[1]))
            vx[c, 0:LP, :] = low(nt(y, wb[2]) + vec[40:41])
            return carry

        lax.fori_loop(0, ncl, features, 0)
        bu = up_bias(vec, 28)
        lane = lax.broadcasted_iota(jnp.int32, (1, 128), 1)
        real = jnp.logical_and(lane >= HEAD0, lane < HEAD0 + 16)
        bias_h = pltpu.roll(jnp.broadcast_to(vec[44:45, 0:128], (8, 128)), HEAD0, 1)[0:1]
        head = low(vec[...])

        def step(chunk, carry):
            clip = (half[0] * count + chunk) // 2
            here = clip - first_clip
            m = mod_rows(mq, vec, 33, clip)
            emb = temb[pl.ds(rank[0] * 8 + clip, 1), :]
            m6, m7 = vec[42:43] + emb, vec[43:44] + emb
            h = jnp.concatenate([h1[chunk, 0], h1[chunk, 1]], axis=0)
            x = h.astype(f32) + jnp.concatenate(
                [jnp.broadcast_to(timing[i : i + 1], (32, h.shape[1])) for i in range(4)], axis=0
            )
            x, kept = self_forward(x, m, wa, (vec[25:26], vec[26:27], vec[27:28]), allowed)
            xb = low(x)
            cq = low(nt(xb, wb[0]) + vec[39:40])
            keys, values = kx[here], vx[here]
            seen = lax.broadcasted_iota(jnp.int32, (1, KP), 1) < lens[clip]
            co, probs = attend(cq, keys, values, seen)
            x = x + (nt(co, wb[3]) + vec[41:42])
            x, kept_f = feed_forward(x, m, wf, bu, vec[32:33])
            h2 = low(x).astype(f32)
            normed, inv = norm(h2)
            cf = low(normed * (1.0 + m7) + m6)
            where = pl.ds(pl.multiple_of(chunk * 128, 128), 128)
            diff = jnp.where(real, nt(cf, head) + bias_h - target[where, :], 0.0)
            scale = errw[pl.ds(clip, 1), 0:1]
            loss[...] += col_sum(diff * diff) * scale
            dpred = low(diff * (2.0 * scale))
            dcf = nn(dpred, head)
            grads[...] += tn(dpred, cf)
            dbh = pltpu.roll(jnp.broadcast_to(col_sum(dpred), (8, 128)), 128 - HEAD0, 1)[0:1]
            grads[44:45, 0:128] += dbh
            dm7, dm6 = col_sum(dcf * normed), col_sum(dcf)
            dx = low(norm_back(dcf * (1.0 + m7), normed, inv)).astype(f32)
            dx, dm_f, db_f, act_f = feed_backward(dx, kept_f, m, wf)
            dcbr = low(dx)
            dco = low(nn(dcbr, wb[3]))
            dcq, dck, dcv = attend_back(dco, cq, keys, values, probs)
            dcq = low(dcq)
            dkv[0, here] += dck[0:LP]
            dkv[1, here] += dcv[0:LP]
            dx = dx + nn(dcq, wb[0])
            dx, dm_a, db_a, act_a = self_backward(dx, kept, m, wa)
            out = low(dx)
            dh1[chunk, 0] = out[0:64]
            dh1[chunk, 1] = out[64:128]
            for i, value in enumerate(act_a + (xb, dcq, co, dcbr)):
                acts[i, where, :] = value
            for i in range(2):
                actf[i, where, :] = act_f[i]
                actw[i, where, :] = act_f[2 + i]
            mods = dm_a + dm_f + (dm6, dm7)
            dmod[chunk] = jnp.concatenate(mods, axis=0)
            for i in range(3):
                grads[25 + i : 26 + i] += db_a[i]
            for i in range(4):
                grads[28 + i : 29 + i] += db_f[0][:, i * 384 : i * 384 + 384]
            grads[32:33] += db_f[1]
            for i in range(6):
                grads[33 + i : 34 + i] += mods[i]
            grads[39:40] += col_sum(dcq)
            grads[41:42] += col_sum(dcbr)
            grads[42:43] += dm6
            grads[43:44] += dm7
            return carry

        lax.fori_loop(0, count, step, 0)


def weight_grad_kernel(
    role, half, rank, acts_s, acts_t, racts, actf_s, actf_t, ractf, actw_s, actw_t, ractw,
    ybuf, rybuf, dkvb, rdkvb, dy, rdy, gq, rgq, hq, y2p, captions,
    own, snd, text_out, la, lf, lw, cap, square, turned, sums, sems,
):
    tokens = acts_s.shape[1]
    line, cols = own.shape[1], own.shape[2]
    odd = lax.rem(rank[0], 2) == 1
    near, far = pl.ds(0, tokens), pl.ds(tokens, tokens)

    def copies(r, h):
        if h == 0:
            local = acts_s if r == 0 else acts_t
            size = pl.ds(0, local.shape[0])
            return [(local, la.at[size, near], 0), (racts.at[size], la.at[size, far], 1)]
        thin, wide = ((actf_s, actw_s), (actf_t, actw_t))[r]
        return [
            (thin, lf.at[:, near], 0), (ractf, lf.at[:, far], 1),
            (wide, lw.at[:, near], 2), (ractw, lw.at[:, far], 3),
        ]

    def text():
        return [(captions.at[c], cap.at[c], 4 + c) for c in range(captions.shape[0])]

    def run(group, finish):
        for src, dst, i in group:
            copy = pltpu.make_async_copy(src, dst, sems.at[i])
            copy.wait() if finish else copy.start()

    for r in range(2):
        for h in range(2):

            @pl.when(jnp.logical_and(role[0] == r, half[0] == h))
            def _():
                run(copies(r, h), False)
                if r == 1:
                    run(text(), False)
                run(copies(r, h), True)

    def keep(unit, at, first, second):
        own[unit, at] = jnp.where(odd, second, first)
        snd[unit, at] = low(jnp.where(odd, first, second))

    def keep_square(unit, value):
        for p in range(line):
            cut = 2 * p * cols
            keep(unit, p, value[cut : cut + cols], value[cut + cols : cut + 2 * cols])

    def matrix(unit, left, right):
        keep_square(unit, tn(la[left], la[right]))

    @pl.when(half[0] == 0)
    def _():
        def square(i, carry):
            left = jnp.where(i < 3, i + 1, 2 * i - 1)
            right = jnp.where(i < 3, 0, 2 * i - 2)
            matrix(jnp.where(i < 5, i, 7), left, right)
            return carry

        lax.fori_loop(0, 4 + 2 * role[0], square, 0)

        @pl.when(role[0] == 1)
        def _():
            def cross(i, carry):
                total = tn(dkvb[i, 0], ybuf[0]) + tn(rdkvb[i, 0], rybuf[0])
                for c in range(1, ybuf.shape[0]):
                    total = total + tn(dkvb[i, c], ybuf[c]) + tn(rdkvb[i, c], rybuf[c])
                keep_square(5 + i, total)
                return carry

            lax.fori_loop(0, 2, cross, 0)

    @pl.when(half[0] == 1)
    def _():
        side = la.shape[2]
        tiles = lw.shape[2] // side
        block = 4 * cols
        per = side // (2 * block)

        def feed(i, carry):
            pair, tile = i // tiles, lax.rem(i, tiles)
            lanes = pl.ds(pl.multiple_of(tile * side, 128), side)
            value = tn(lw[pair, :, lanes], lf[pair])
            for p in range(per):
                for j in range(4):
                    at = 2 * p * block + j * cols
                    keep(
                        4 * pair + j, tile * per + p, value[at : at + cols],
                        value[at + block : at + block + cols],
                    )
            return carry

        lax.fori_loop(0, 2 * tiles, feed, 0)

    @pl.when(role[0] == 1)
    def _():
        clips = captions.shape[0]
        rows = captions.shape[1]
        def dy_of(c):
            h = (2 * c) // clips
            at = c - (h * clips) // 2
            return jnp.where(half[0] == h, dy[at].astype(f32), rdy[at].astype(f32)).astype(bf16)

        @pl.when(half[0] == 1)
        def _():
            shape = (y2p.shape[2], y2p.shape[1], cols)
            mine, theirs = units_of(1, *shape), units_of(0, *shape)
            square[...] = jnp.zeros_like(square)

            def one(c, carry):
                plain = low(nn(gq[c], mine) + nn(rgq[c], theirs))
                square[...] += tn(dy_of(c), plain)
                return carry

            lax.fori_loop(0, clips, one, 0)
            keep_square(8, square[...])

        units = text_out.shape[2]

        def keep_text(lanes, value):
            for p in range(line):
                for q in range(2):
                    cut = (2 * p + q) * units
                    text_out[p, q, :, lanes] = low(value[cut : cut + units])

        ones = jnp.ones((LP, 128), bf16)
        sums[...] = jnp.zeros_like(sums)

        def turn(c, carry):
            back = nn(dy_of(c), y2p[half[0]]) * gelu_both(hq[c])[1]
            turned[c] = low(jnp.transpose(back))
            sums[...] += nn(turned[c], ones)
            return carry

        lax.fori_loop(0, clips, turn, 0)
        run(text(), True)

        def text_tile(t, carry):
            lanes = pl.ds(pl.multiple_of(t * 512, 512), 512)
            total = nn(turned[0, :, 0:rows], cap[0, :, lanes])
            for c in range(1, clips):
                total = total + nn(turned[c, :, 0:rows], cap[c, :, lanes])
            keep_text(lanes, total)
            return carry

        lax.fori_loop(0, captions.shape[2] // 512, text_tile, 0)
        keep_text(pl.ds(captions.shape[2], 128), sums[...])


def halves(value):
    first = low(value)
    return first, low(value - first.astype(f32))


def lefts(value, axis=1):
    first, second = halves(value)
    return jnp.concatenate([first, first, second], axis=axis)


def rights(value, axis=0):
    first, second = halves(value)
    return jnp.concatenate([first, second, first], axis=axis)


def gram_of(value, dot):
    first, second = halves(value)
    both = dot(first, first), dot(first, second)
    return both[0] + (both[1] + jnp.transpose(both[1]))


def muon_kernel(half, ua, uf, xa, xf, gram, whole):
    @pl.when(half[0] == 0)
    def _():
        u = ua[...]
        whole[...] = u / (jnp.sqrt(jnp.sum(u * u)) + 1e-07)

        def sweep(i, carry):
            x = whole[...]
            square = gram_of(x, nt)
            poly = coef_b * square + coef_c * gram_of(square, nt)
            whole[...] = coef_a * x + nn(lefts(poly), rights(x))
            return carry

        lax.fori_loop(0, 5, sweep, 0)
        xa[...] = low(whole[...])

    @pl.when(half[0] == 1)
    def _():
        width = uf.shape[1]
        tiles = uf.shape[0] // width
        gram[...] = jnp.zeros_like(gram)

        def rows(t):
            return pl.ds(pl.multiple_of(t * width, 128), width)

        def first(t, carry):
            piece = uf[rows(t), :]
            gram[...] += gram_of(piece, tn)
            return carry

        lax.fori_loop(0, tiles, first, 0)
        row = lax.broadcasted_iota(jnp.int32, (width, width), 0)
        col = lax.broadcasted_iota(jnp.int32, (width, width), 1)
        eye = jnp.where(row == col, 1.0, 0.0)
        start = gram[...]
        inv = 1.0 / (jnp.sqrt(jnp.sum(start * eye)) + 1e-07)
        gram[...] = start * (inv * inv)
        whole[...] = eye * inv

        def poly_of(a):
            return coef_a * eye + coef_b * a + coef_c * nn(lefts(a), rights(a))

        def sweep(i, carry):
            a = gram[...]
            left = lefts(poly_of(a))
            both = nn(left, rights(jnp.concatenate([a, whole[...]], axis=1)))
            whole[...] = both[:, width:]

            @pl.when(i < 4)
            def _():
                gram[...] = nn(left, rights(both[:, :width]))

            return carry

        lax.fori_loop(0, 5, sweep, 0)
        last = rights(whole[...])

        def apply(t, carry):
            xf[rows(t), :] = low(nn(lefts(uf[rows(t), :]), last))
            return carry

        lax.fori_loop(0, tiles, apply, 0)


def local_call(kernel, out_shape, in_specs, args, scratch=(), out_specs=None):
    return pl.pallas_call(
        kernel,
        out_shape=out_shape,
        in_specs=in_specs,
        out_specs=jax.tree.map(lambda _: VM, out_shape) if out_specs is None else out_specs,
        scratch_shapes=scratch,
        compiler_params=pltpu.CompilerParams(vmem_limit_bytes=VMEM_LIMIT),
    )(*args)


def here():
    return lax.axis_index("dp"), lax.axis_index("segment")


def dev(d, s):
    return {"dp": d, "segment": s}


def remote(src, dst, send, recv, target):
    return pltpu.make_async_remote_copy(
        src_ref=src, dst_ref=dst, send_sem=send, recv_sem=recv, device_id=target,
        device_id_type=MESH,
    )


def greet(targets):
    barrier = pltpu.get_barrier_semaphore()
    for target in targets:
        pl.semaphore_signal(barrier, inc=1, device_id=target, device_id_type=MESH)
    pl.semaphore_wait(barrier, len(targets))


def greet_dp(n, extra=()):
    d, s = here()
    barrier = pltpu.get_barrier_semaphore()

    def step(k, carry):
        pl.semaphore_signal(
            barrier, inc=1, device_id=dev(lax.rem(d + k, n), s), device_id_type=MESH
        )
        return carry

    lax.fori_loop(1, n, step, 0)
    for target in extra:
        pl.semaphore_signal(barrier, inc=1, device_id=target, device_id_type=MESH)
    pl.semaphore_wait(barrier, n - 1 + len(extra))


def comm_call(kernel, cid, args, out_shape, sems, out_specs=None, scratch=(), in_specs=None):
    if out_specs is None:
        out_specs = jax.tree.map(lambda _: ANY, out_shape)
    return pl.pallas_call(
        kernel,
        out_shape=out_shape,
        in_specs=[ANY] * len(args) if in_specs is None else in_specs,
        out_specs=out_specs,
        scratch_shapes=list(scratch) + [pltpu.SemaphoreType.DMA(shape) for shape in sems],
        compiler_params=pltpu.CompilerParams(
            collective_id=cid, has_side_effects=True, vmem_limit_bytes=VMEM_LIMIT
        ),
    )(*args)


def gather_kernel(n, pa, pb, pf, pw, py, pm, pt, wa, wb, wf, ww, wy, wm, wt,
                  send, recv, crecv, own):
    pair = 2 if n % 2 == 0 else 1
    line = n // pair
    d, s = here()
    role, half = s // 2, lax.rem(s, 2)
    a, x = d // pair, lax.rem(d, pair)
    mate = dev(d, role * 2 + 1 - half)
    above, below = dev(d + pair, s), dev(d - pair, s)
    across = dev(a * pair + (pair - 1 - x), s)
    barrier = pltpu.get_barrier_semaphore()

    def signal(target):
        pl.semaphore_signal(barrier, inc=1, device_id=target, device_id_type=MESH)

    signal(mate)
    if pair == 2:
        signal(across)

    @pl.when(a < line - 1)
    def _():
        signal(above)

    @pl.when(a > 0)
    def _():
        signal(below)

    pl.semaphore_wait(barrier, pair + jnp.minimum(a, 1) + jnp.minimum(line - 1 - a, 1))

    def two(i, ref, out):
        return [
            (i, ref.at[pl.ds(0, 2)], out.at[pl.ds(0, 2)], 2),
            (i + 1, ref.at[pl.ds(2, 2)], out.at[pl.ds(2, 2)], 2),
        ]

    first, last = half == 0, role == 1
    both = jnp.logical_and(first, last)
    shared = [((2, pw, ww, 0), first, True)]
    shared += [(item, first, True) for item in two(0, pa, wa)]
    shared += [(item, both, last) for item in two(5, pb, wb)]
    for m in range(2):
        item = (m, pf.at[pl.ds(m, 1)], wf.at[pl.ds(m, 1)], 1)
        shared.append((item, jnp.logical_not(first), True))
    alone = [((3, pt, wt, 0), True), ((4, pm, wm, 0), role == 0), ((4, py, wy, 0), role == 1)]
    parts = [(item, when, True) for item, when, _ in shared]
    parts += [(item, when, False) for item, when in alone]

    def slot(ref, lead, o):
        return ref.at[:, o] if lead else ref.at[o]

    def given(when, act):
        if when is True:
            act()
        else:
            pl.when(when)(act)

    def move(item, way, o, target, is_own=False):
        i, src, dst, lead = item
        there = slot(dst, lead, o)
        sem = crecv if way == 3 else recv
        return remote(src if is_own else there, there, send.at[way, i, o], sem.at[i, o], target)

    def forward(o, up, down, side, wait):
        is_own = not wait
        for item, when, common in parts:

            def act(item=item, common=common):
                if wait:
                    move(item, 0, o, across).wait_recv()

                def go(way, target):
                    move(item, way, o, target, is_own).start()

                if side and pair == 2:
                    go(2, across)
                if up is not None:
                    pl.when(up)(functools.partial(go, 0, above))
                if down is not None:
                    pl.when(down)(functools.partial(go, 1, below))
                if common:
                    go(3, mate)

            given(when, act)

    def keep(finish):
        for item, when, common in parts:

            def act(item=item):
                i, src, dst, lead = item
                copy = pltpu.make_async_copy(src, slot(dst, lead, d), own.at[i])
                copy.wait() if finish else copy.start()

            given(when, act)

    forward(d, a < line - 1, a > 0, True, False)
    keep(False)
    other = pair - 1 - x

    def sweep():
        def step(k, carry):
            @pl.when(a - k >= 0)
            def _():
                forward((a - k) * pair + x, a < line - 1, None, True, True)

            @pl.when(a + k < line)
            def _():
                forward((a + k) * pair + x, None, a > 0, True, True)

            if pair == 2:

                def from_side(o, carry):
                    forward(o * pair + other, None, None, False, True)
                    return carry

                @pl.when(a - (k - 1) >= 0)
                def _():
                    from_side(a - (k - 1), 0)

                @pl.when(jnp.logical_and(k > 1, a + (k - 1) < line))
                def _():
                    from_side(a + (k - 1), 0)

            return carry

        lax.fori_loop(1, line + 1, step, 0)

    sweep()

    def drain(o, carry):
        there, column = o // pair, lax.rem(o, pair)
        mine = column == x
        sent = (
            (0, jnp.logical_and(mine, jnp.logical_and(there <= a, a < line - 1)), above),
            (1, jnp.logical_and(mine, jnp.logical_and(there >= a, a > 0)), below),
            (2, mine, across),
        )
        for item, when, common in parts:

            def act(item=item, common=common):
                for way, yes, target in sent:
                    if way == 2 and pair == 1:
                        continue
                    pl.when(yes)(lambda: move(item, way, o, target).wait_send())
                if common:
                    move(item, 3, o, mate).wait_send()

            given(when, act)
        return carry

    lax.fori_loop(0, n, drain, 0)
    keep(True)

    def collect(o, carry):
        for item, when, arrives in shared:
            mine = when if when is not both else first

            def act(item=item):
                i, src, dst, lead = item
                there = slot(dst, lead, o)
                remote(there, there, send.at[3, i, o], crecv.at[i, o], mate).wait_recv()

            given(jnp.logical_and(jnp.logical_not(mine), arrives), act)
        return carry

    lax.fori_loop(0, n, collect, 0)


def mate_kernel(src, dst, send, recv, own):
    d, s = here()
    role, half = s // 2, lax.rem(s, 2)
    mate = dev(d, role * 2 + 1 - half)

    @pl.when(role == 0)
    def _():
        greet([mate])
        pltpu.make_async_copy(src, dst.at[half], own.at[0]).start()
        remote(src, dst.at[half], send.at[0], recv.at[0], mate).start()
        pltpu.make_async_copy(src, dst.at[half], own.at[0]).wait()
        remote(src, dst.at[1 - half], send.at[0], recv.at[0], mate).wait()


def forward_kernel(count, h1s, gq, mq, h1t, gqs, mqt, send, recv, msend, mrecv, qsend, qrecv):
    relay_half_clips(
        count, 0, h1s, h1t, send, recv, swap=(gq, gqs, msend, mrecv), rows=(mq, mqt, qsend, qrecv)
    )


def relay_half_clips(count, from_role, src, dst, send, recv, extra=None, swap=None, rows=None):
    d, s = here()
    role, half = s // 2, lax.rem(s, 2)
    peers = [dev(d, (1 - role) * 2), dev(d, (1 - role) * 2 + 1)]
    mate = dev(d, role * 2 + 1 - half)
    peers.append(mate)
    greet(peers)

    def unit(i, part):
        there = half * count + i
        clip, own = there // 2, lax.rem(there, 2)
        other = 2 * clip + part
        return own, other // count, lax.rem(other, count)

    def copy(i, part):
        own, to, slot = unit(i, part)
        return remote(
            src.at[i, part], dst.at[slot, own], send.at[i, part], recv.at[slot, own],
            dev(d, (1 - from_role) * 2 + to),
        )

    def row_copy(to, finish):
        value, there, qsend, qrecv = rows
        slot = there.at[half] if from_role == 1 else there
        copy = remote(value, slot, qsend.at[to], qrecv.at[half], dev(d, (1 - from_role) * 2 + to))
        copy.wait_send() if finish else copy.start()

    def row_sends(finish):
        if rows is None:
            return

        @pl.when(role == from_role)
        def _():
            if from_role == 0:
                for to in range(2):
                    pl.when(half == to)(functools.partial(row_copy, to, finish))
            else:
                for to in range(2):
                    row_copy(to, finish)

    row_sends(False)
    if swap is not None:
        mine, both, msend, mrecv = swap

        @pl.when(role == 1)
        def _():
            remote(mine, both, msend.at[0], mrecv.at[0], mate).start()

    if extra is not None:
        own_src, own_dst, esend, erecv = extra

        @pl.when(jnp.logical_and(role == 1, half == 1))
        def _():
            remote(own_src, own_dst, esend.at[0], erecv.at[0], dev(d, 2)).start()

    @pl.when(role == from_role)
    def _():
        for i in range(count):
            for part in range(2):
                copy(i, part).start()
        for i in range(count):
            for part in range(2):
                copy(i, part).wait_send()

    @pl.when(role == 1 - from_role)
    def _():
        for i in range(count):
            for part in range(2):
                remote(
                    src.at[i, part], dst.at[i, part], send.at[i, part], recv.at[i, part],
                    dev(d, from_role * 2),
                ).wait_recv()

    row_sends(True)
    if rows is not None:
        value, there, qsend, qrecv = rows

        @pl.when(role == 1 - from_role)
        def _():
            if from_role == 0:
                remote(value, there, qsend.at[0], qrecv.at[half], mate).wait_recv()
            else:
                for o in range(2):
                    remote(value, there.at[o], qsend.at[0], qrecv.at[o], mate).wait_recv()

    if swap is not None:

        @pl.when(role == 1)
        def _():
            remote(mine, both, msend.at[0], mrecv.at[0], mate).wait()

    if extra is not None:

        @pl.when(jnp.logical_and(role == 1, half == 1))
        def _():
            remote(own_src, own_dst, esend.at[0], erecv.at[0], dev(d, 2)).wait_send()

        @pl.when(jnp.logical_and(role == 1, half == 0))
        def _():
            remote(own_src, own_dst, esend.at[0], erecv.at[0], dev(d, 2)).wait_recv()


def backward_kernel(count, dh1, dkv, dmod, dhs, extra, dmods, send, recv, esend, erecv, qsend,
                    qrecv):
    relay_half_clips(
        count, 1, dh1, dhs, send, recv, extra=(dkv.at[:, 0], extra, esend, erecv),
        rows=(dmod, dmods, qsend, qrecv),
    )


def swap_kernel(acts_s, acts_t, actf_s, actf_t, actw_s, actw_t, ybuf, dkvb, dy, dmod,
                racts, ractf, ractw, rybuf, rdkvb, rdy, rdmod, send, recv):
    d, s = here()
    role, half = s // 2, lax.rem(s, 2)
    mate = dev(d, role * 2 + 1 - half)
    greet([mate])
    six = acts_s.shape[0]
    gives = {
        (0, 0): [(0, actf_s, ractf), (1, actw_s, ractw), (4, dmod, rdmod)],
        (0, 1): [(0, acts_s, racts.at[pl.ds(0, six)]), (4, dmod, rdmod)],
        (1, 0): [(0, actf_t, ractf), (1, actw_t, ractw), (2, dy, rdy)],
        (1, 1): [(0, acts_t, racts), (1, ybuf, rybuf), (3, dkvb, rdkvb), (2, dy, rdy)],
    }
    for (r, h), mine in gives.items():

        @pl.when(jnp.logical_and(role == r, half == h))
        def _():
            for i, src, dst in mine:
                remote(src, dst, send.at[i], recv.at[i], mate).start()
            for i, src, dst in mine:
                remote(src, dst, send.at[i], recv.at[i], mate).wait_send()
            for i, src, dst in gives[(r, 1 - h)]:
                remote(src, dst, send.at[i], recv.at[i], mate).wait_recv()


TEXT_CUTS = 11


def scatter_kernel(n, own_in, snd, text_in, dm, vec, loss, wm, temb, ww, hid, wt,
                   summed, text, vsum, squares, gm, g2, g1,
                   own, rx, up, down, sx, rz, tin, trx, tsx, trz, rv, rm, dtembs,
                   osem, send1, recv1, send2, recv2, usend, urecv, dsend, drecv,
                   ssend, srecv, sown, tsend, trecv, esend, erecv):
    line = n // 2
    d, s = here()
    role, half = s // 2, lax.rem(s, 2)
    a, x = d // 2, lax.rem(d, 2)
    across = dev(a * 2 + 1 - x, s)
    other = dev(d, (1 - role) * 2 + half)
    count = 8 - 4 * (1 - role) * (1 - half)
    greet_dp(n, [other])
    squares[...] = jnp.zeros_like(squares)
    squares[1:2, 0:128] = loss[...]
    step = text.shape[1] // TEXT_CUTS
    is_text, is_last, is_time = role == 0, s == 3, s == 0
    clip_rows = dm.shape[0]

    def first_copies(u):
        return (
            remote(snd.at[u], rx.at[u], send1.at[u], recv1.at[u], across),
            pltpu.make_async_copy(own_in.at[u], own.at[u], osem.at[u]),
        )

    def text_hop(k):
        lanes = pl.ds(pl.multiple_of(k * step, 128), step)
        return remote(text_in.at[:, :, :, lanes], tin.at[k], tsend.at[k], trecv.at[k], other)

    def text_across(k):
        return remote(tin.at[k, :, 1 - x], trx.at[k], send1.at[9 + k], recv1.at[9 + k], across)

    def begin(u, carry):
        for copy in first_copies(u):
            copy.start()
        return carry

    def rows_at(o):
        return rm.at[pl.ds(pl.multiple_of(o * clip_rows, 8), clip_rows)]

    def small(i, finish):
        src, dst = (
            (lambda p: vec.at[p], lambda o: rv.at[o]) if i else (lambda p: dm, rows_at)
        )

        def each(k, carry):
            to, o = lax.rem(d + k, n), lax.rem(d + n - k, n)
            if finish:
                remote(src(o), dst(o), ssend.at[i, k], srecv.at[i, k], dev(o, s)).wait()
            else:
                remote(src(to), dst(d), ssend.at[i, k], srecv.at[i, k], dev(to, s)).start()
            return carry

        lax.fori_loop(1, n, each, 0)
        copy = pltpu.make_async_copy(src(d), dst(d), sown.at[i])
        copy.wait() if finish else copy.start()

    pl.when(is_time)(lambda: small(0, False))
    lax.fori_loop(0, 1, begin, 0)
    small(1, False)
    lax.fori_loop(1, count, begin, 0)

    @pl.when(is_last)
    def _():
        begin(8, 0)

    @pl.when(role == 1)
    def _():
        lax.fori_loop(0, TEXT_CUTS, lambda k, c: (text_hop(k).start(), c)[1], 0)

    def embeds(finish):
        def each(k, carry):
            to, o = lax.rem(d + k, n), lax.rem(d + n - k, n)
            if finish:
                remote(dtembs.at[o], dtembs.at[o], esend.at[k], erecv.at[k], dev(o, s)).wait()
            else:
                remote(dtembs.at[d], dtembs.at[d], esend.at[k], erecv.at[k], dev(to, s)).start()
            return carry

        lax.fori_loop(1, n, each, 0)

    def upward(u, p):
        return remote(up.at[u, p], up.at[u, p], usend.at[u, p], urecv.at[u, p], dev(d + 2, s))

    def downward(u, p):
        return remote(
            down.at[u, p], down.at[u, p], dsend.at[u, p], drecv.at[u, p], dev(d - 2, s)
        )

    def along_up(u):
        def add(i, carry):
            p = line - 1 - i

            @pl.when(a == 0)
            def _():
                up[u, p] = own[u, p]

            @pl.when(a > 0)
            def _():
                upward(u, p).wait_recv()
                up[u, p] = up[u, p] + own[u, p]

            return carry

        def send(i, carry):
            upward(u, line - 1 - i).start()
            return carry

        lax.fori_loop(0, line - 1 - a, add, 0)
        lax.fori_loop(0, line - 1 - a, send, 0)

    def along_down(u):
        def add(p, carry):
            @pl.when(a == line - 1)
            def _():
                down[u, p] = own[u, p]

            @pl.when(a < line - 1)
            def _():
                downward(u, p).wait_recv()
                down[u, p] = down[u, p] + own[u, p]

            return carry

        def send(p, carry):
            downward(u, p).start()
            return carry

        lax.fori_loop(0, a, add, 0)
        lax.fori_loop(0, a, send, 0)

    def pairs(u):
        for copy in first_copies(u):
            copy.wait()
        own[u] = own[u] + rx[u].astype(f32)

    def direct(i, total, line_in, finish):
        def each(k, carry):
            to, o = lax.rem(a + k, line), lax.rem(a + line - k, line)
            if finish:
                remote(
                    total.at[o], line_in.at[o], send2.at[i, k], recv2.at[i, k], dev(o * 2 + x, s)
                ).wait()
            else:
                remote(
                    total.at[to], line_in.at[a], send2.at[i, k], recv2.at[i, k],
                    dev(to * 2 + x, s),
                ).start()
            return carry

        lax.fori_loop(1, line, each, 0)

    def round_trip(i, carry):
        @pl.when(i < count)
        def _():
            pairs(i)

        @pl.when(jnp.logical_and(is_time, i == 1))
        def _():
            small(0, True)
            time_back([d], rm, wm, temb, dtembs.at[d])

        pl.when(jnp.logical_and(is_time, i == 2))(lambda: embeds(False))

        @pl.when(is_text)
        def _():
            def cut_at(delay, act):
                k = i - delay
                pl.when(jnp.logical_and(k >= 0, k < TEXT_CUTS))(lambda: act(k))

            def arrive(k):
                text_hop(k).wait_recv()
                text_across(k).start()

            def add(k):
                text_across(k).wait()
                tsx[k] = low(tin[k, :, x].astype(f32) + trx[k].astype(f32))

            cut_at(4, lambda k: direct(k, tsx.at[k], trz.at[k], False))
            cut_at(1, arrive)
            cut_at(3, add)

        k = i - count

        @pl.when(jnp.logical_and(is_last, k == 0))
        def _():
            pairs(8)
            sx[...] = low(own[8])

        @pl.when(jnp.logical_and(is_last, k == 1))
        def _():
            direct(TEXT_CUTS, sx, rz, False)

        later = i - 1 - a

        @pl.when(jnp.logical_and(later >= 0, later < count))
        def _():
            along_up(later)

        other = i - line + a

        @pl.when(jnp.logical_and(other >= 0, other < count))
        def _():
            along_down(other)

        return carry

    lax.fori_loop(0, jnp.maximum(count + line, TEXT_CUTS + 4), round_trip, 0)
    small(1, True)
    vsum[...] = lax.fori_loop(0, n, lambda o, total: total + rv[o], jnp.zeros(vsum.shape, f32))

    @pl.when(is_time)
    def _():
        embeds(True)
        time_grad([d], rm, dtembs, ww, temb, hid, wt, gm, g2, g1, vsum, squares)

    @pl.when(role == 1)
    def _():
        lax.fori_loop(0, TEXT_CUTS, lambda k, c: (text_hop(k).wait_send(), c)[1], 0)

    def collect(u, carry):
        @pl.when(a > 0)
        def _():
            upward(u, a).wait_recv()
            own[u, a] = own[u, a] + up[u, a]

        @pl.when(a < line - 1)
        def _():
            downward(u, a).wait_recv()
            own[u, a] = own[u, a] + down[u, a]

        whole = own[u, a]
        summed[u] = whole
        squares[0:1, :] += col_sum(whole * whole)
        return carry

    lax.fori_loop(0, count, collect, 0)

    def drain(u, carry):
        def one(i, c):
            upward(u, line - 1 - i).wait_send()
            return c

        def two(p, c):
            downward(u, p).wait_send()
            return c

        lax.fori_loop(0, line - 1 - a, one, 0)
        lax.fori_loop(0, a, two, 0)
        return carry

    lax.fori_loop(0, count, drain, 0)

    def others(line_in, whole):
        return lax.fori_loop(
            1, line, lambda k, acc: acc + line_in[lax.rem(a + k, line)].astype(f32), whole
        )

    @pl.when(is_last)
    def _():
        direct(TEXT_CUTS, sx, rz, True)
        whole = others(rz, own[8, a])
        summed[8] = whole
        squares[0:1, :] += col_sum(whole * whole)

    @pl.when(is_text)
    def _():
        def whole_cut(k, carry):
            direct(k, tsx.at[k], trz.at[k], True)
            whole = others(trz.at[k], tin[k, a, x].astype(f32) + trx[k, a].astype(f32))
            text[:, pl.ds(pl.multiple_of(k * step, 128), step)] = low(whole)
            lane = lax.broadcasted_iota(jnp.int32, (1, step), 1)
            spare = jnp.logical_and(k == TEXT_CUTS - 1, lane > step - 128)
            counted = jnp.where(spare, 0.0, whole)
            squares[0:1, :] += col_sum(counted * counted)
            return carry

        lax.fori_loop(0, TEXT_CUTS, whole_cut, 0)


def three(value):
    first = low(value)
    rest = value - first.astype(f32)
    second = low(rest)
    return first, second, low(rest - second.astype(f32))


def nn3(left, right):
    return sum(nn(piece, right) for piece in three(left))


def nt3(left, right):
    return sum(nt(piece, right) for piece in three(left))


def tn3(left, right):
    return sum(tn(left, piece) for piece in three(right))


def own_columns(rank, width, cols):
    row = lax.broadcasted_iota(jnp.int32, (width, 128), 0)
    col = lax.broadcasted_iota(jnp.int32, (width, 128), 1)
    return low(jnp.where(jnp.logical_and(row == rank * cols + col, col < cols), 1.0, 0.0))


def clip_groups(clips, rows):
    per = 8 * (rows // (clips // 8) // 8)
    left = lax.broadcasted_iota(jnp.int32, (clips, rows), 0)
    right = lax.broadcasted_iota(jnp.int32, (clips, rows), 1)
    match = (right // per) * 8 + (right % per) // 8 == left
    return low(jnp.where(match, 1.0, 0.0))


def silu_back(value):
    gate = jax.nn.sigmoid(value)
    return gate * (1.0 + value * (1.0 - gate))


def time_back(rank, rm, wm, temb, dtemb):
    cols, width = wm.shape[0], rm.shape[1]
    rows, clips = rm.shape[0], temb.shape[0]
    pick = own_columns(rank[0], width, cols)
    kind = lax.broadcasted_iota(jnp.int32, (rows, 1), 0) % 8
    value = rm[...]
    pieces = three(value)
    total = jnp.where(kind >= 6, nn3(value, pick), 0.0)
    zeros = jnp.zeros((128 - cols, width), bf16)

    def one(r, total):
        lanes = pl.ds(pl.multiple_of(r * width, 128), width)
        weight = jnp.concatenate([wm[:, lanes], zeros], axis=0)
        back = nt(pieces[0], weight) + nt(pieces[1], weight) + nt(pieces[2], weight)
        return total + jnp.where(kind == r, back, 0.0)

    total = lax.fori_loop(0, 6, one, total)
    slope = silu_back(nn3(temb[...], pick))
    group = clip_groups(clips, rows)

    def collapse(part):
        first, second, third = three(part)
        return nn(group, first) + nn(group, second) + nn(group, third)

    dtemb[...] = collapse(jnp.where(kind < 6, total, 0.0)) * slope + collapse(
        jnp.where(kind >= 6, total, 0.0)
    )


def time_grad(rank, rm, dtembs, ww, temb, hid, wt, gm, g2, g1, vout, tout):
    width, cols = rm.shape[1], vout.shape[0]
    rows, clips = rm.shape[0], temb.shape[0]
    n = dtembs.shape[0]
    pick = own_columns(rank[0], width, cols)
    kind = lax.broadcasted_iota(jnp.int32, (rows, 1), 0) % 8
    value = rm[...]
    hidden = hid[...]
    own_hid, own_temb = nn3(hidden, pick), nn3(temb[...], pick)
    gates = low(own_temb * jax.nn.sigmoid(own_temb))
    spread = low(tn(clip_groups(clips, rows), gates))
    pieces = three(value)
    count = jnp.zeros((1, 1), f32)

    def squared(block):
        return jnp.sum(jnp.sum(block * block, axis=1, keepdims=True), axis=0, keepdims=True)

    def one(r, count):
        masked = jnp.where(kind == r, spread.astype(f32), 0.0).astype(bf16)
        block = sum(tn(masked, piece) for piece in pieces)[0:cols]
        gm[:, pl.ds(pl.multiple_of(r * width, 128), width)] = block
        return count + squared(block)

    count = lax.fori_loop(0, 6, one, count)
    mine = dtembs[rank[0]]
    mine_pieces = three(mine)
    act = low(hidden * jax.nn.sigmoid(hidden))
    block = sum(tn(piece, act) for piece in mine_pieces)[0:cols]
    g2[...] = block
    count = count + squared(block)
    back = jnp.zeros((clips, 128), f32)
    zeros = jnp.zeros((128 - cols, 128), bf16)
    picked = low(nn(ww[:, 256 : 256 + width], pick))
    for o in range(n):
        weight = picked[o * cols : o * cols + cols]
        back = back + nn3(dtembs[o], jnp.concatenate([weight, zeros], axis=0))
    dhid = back * silu_back(own_hid)
    dhid_pieces = three(dhid)
    feature = low(wt[:, 0:256])
    block = sum(tn(piece, feature) for piece in dhid_pieces)[0:cols]
    g1[...] = block
    count = count + squared(block)
    at = lax.broadcasted_iota(jnp.int32, (clips, 128), 1)
    first = low(jnp.where(at == 1, 1.0, 0.0))
    second = low(jnp.where(at == 2, 1.0, 0.0))
    total = sum(tn(piece, first) for piece in dhid_pieces)
    total = total + sum(tn(piece, second) for piece in mine_pieces)
    row_kind = lax.broadcasted_iota(jnp.int32, (rows, 128), 0) % 8
    row_lane = lax.broadcasted_iota(jnp.int32, (rows, 128), 1)
    put = jnp.logical_and(row_lane == row_kind + 3, row_kind < 6)
    put = low(jnp.where(put, 1.0, 0.0))
    total = total + sum(tn(piece, put) for piece in three(nn3(value, pick)))

    vout[...] += total[0:cols]
    lane = lax.broadcasted_iota(jnp.int32, (1, 128), 1)
    tout[0:1, 0:128] += jnp.where(lane == 0, count, 0.0)


class Relay:
    def __init__(self, send, recv):
        self.d, self.s = here()
        self.role, self.half = self.s // 2, lax.rem(self.s, 2)
        self.other = dev(self.d, (1 - self.role) * 2 + self.half)
        self.mate = dev(self.d, self.role * 2 + 1 - self.half)
        self.send, self.recv = send, recv

    def at(self, r, h):
        return jnp.logical_and(self.role == r, self.half == h)

    def copy(self, i, leg, src, dst):
        target = self.other if leg == 0 else self.mate
        return remote(src, dst, self.send.at[i, leg], self.recv.at[i, leg], target)

    def start(self, i, src, dst):
        self.copy(i, 0, src, dst).start()
        self.copy(i, 1, src, dst).start()

    def middle(self, i, dst):
        self.copy(i, 0, dst, dst).wait_recv()
        self.copy(i, 2, dst, dst).start()

    def finish(self, r, h, items):
        @pl.when(self.at(r, h))
        def _():
            for i, src, dst in items:
                self.copy(i, 0, src, dst).wait_send()
                self.copy(i, 1, src, dst).wait_send()

        @pl.when(self.at(1 - r, h))
        def _():
            for i, src, dst in items:
                self.copy(i, 2, dst, dst).wait_send()

        @pl.when(self.at(r, 1 - h))
        def _():
            for i, src, dst in items:
                self.copy(i, 1, dst, dst).wait_recv()

        @pl.when(self.at(1 - r, 1 - h))
        def _():
            for i, src, dst in items:
                self.copy(i, 2, dst, dst).wait_recv()


def owner_first(role, mat):
    return 2 * mat + mat % 2 if role == 0 else mat


def owner_second(mat):
    return 2 + 3 * mat


def settle_kernel(n, vsum, tile, summed, att_m, feed_m, gm, g2, g1,
                  oa, of, xa, xf, xm, x2, x1, gv, stat,
                  vecs, tiles, mine, totals, look, mom,
                  msem, send, recv, own, gsend, grecv, gown, ssend, srecv, tsend, trecv):
    relay = Relay(gsend, grecv)
    d, s, role, half = relay.d, relay.s, relay.role, relay.half
    peers = [dev(d, lax.rem(s + k, 4)) for k in range(1, 4)]
    greet_dp(n, peers)
    four, eight = pl.ds(0, 4), pl.ds(0, 8)
    shared = {
        (0, 0): [(0, summed.at[four], xa.at[four]), (4, gm, xm), (5, g2, x2), (6, g1, x1)],
        (0, 1): [(1, summed.at[eight], xf.at[eight])],
        (1, 0): [(2, summed.at[eight], xa.at[pl.ds(4, 8)])],
        (1, 1): [(3, summed.at[eight], xf.at[pl.ds(8, 8)])],
    }
    def momentum(finish):
        sources = {
            (0, 0): (att_m.at[four], mom.at[four]),
            (0, 1): (feed_m.at[eight], mom),
            (1, 0): (att_m.at[pl.ds(4, 8)], mom),
            (1, 1): (feed_m.at[pl.ds(8, 8)], mom),
        }
        for (r, h), (src, dst) in sources.items():

            @pl.when(relay.at(r, h))
            def _():
                copy = pltpu.make_async_copy(src, dst, msem.at[0])
                copy.wait() if finish else copy.start()

    momentum(False)
    small = [(0, vsum, vecs), (1, tile, tiles)]
    for i, src, dst in small:
        for k in range(1, 4):
            remote(src, dst.at[s], ssend.at[i, k], srecv.at[i, k], peers[k - 1]).start()
    for (r, h), items in shared.items():

        @pl.when(relay.at(r, h))
        def _():
            for i, src, dst in items:
                pltpu.make_async_copy(src, dst, gown.at[i]).start()
                relay.start(i, src, dst)

    total, squares, losses = vsum[...], tile[0:1, :], tile[1:2, :]
    for k in range(1, 4):
        o = lax.rem(s + 4 - k, 4)
        for i, src, dst in small:
            remote(src, dst.at[o], ssend.at[i, k], srecv.at[i, k], dev(d, o)).wait()
        total = total + vecs[o]
        squares = squares + tiles[o, 0:1, :]
        losses = losses + tiles[o, 1:2, :]
    lane = lax.broadcasted_iota(jnp.int32, (1, 128), 1)
    total = jnp.where(jnp.logical_or(lane == 9, lane >= 77), 0.0, total)
    gv[...] = total

    def whole(block):
        return jnp.sum(jnp.sum(block, axis=1, keepdims=True), axis=0, keepdims=True)

    row = lax.broadcasted_iota(jnp.int32, (8, 128), 0)
    mine[...] = jnp.where(row < 4, whole(squares) + whole(total * total), whole(losses[:, 0:128]))
    so_far = mine[...]

    def start(k, carry):
        remote(mine, totals.at[d], tsend.at[k], trecv.at[k], dev(lax.rem(d + k, n), s)).start()
        return carry

    lax.fori_loop(1, n, start, 0)

    def finish(k, carry):
        o = lax.rem(d + n - k, n)
        remote(mine, totals.at[o], tsend.at[k], trecv.at[k], dev(o, s)).wait()
        return carry + totals[o]

    lax.fori_loop(1, n, lambda k, c: (finish(k, so_far), c)[1], 0)
    totals[d] = so_far
    so_far = lax.fori_loop(0, n, lambda o, c: c + totals[o], jnp.zeros((8, 128), f32))
    stat[...] = so_far
    factor = jnp.minimum(1.0, max_norm / (jnp.sqrt(so_far[0:1, 0:1]) + 1e-06))
    scale = factor * (1.0 + momentum_decay)

    momentum(True)

    def update(m, carry):
        look[m] = summed[m] * scale + mom[m] * (momentum_decay * momentum_decay)
        return carry

    lax.fori_loop(0, 8, update, 0)
    groups = []
    for r in range(2):
        mats = 4 if r == 0 else 8
        groups.append((r, 0, [(m, owner_first(r, m), look.at[m], oa) for m in range(mats)]))
        groups.append((
            r, 1, [(m, owner_second(m), look.at[pl.ds(4 * m, 4)], of) for m in range(2)]
        ))
    for r, h, mats in groups:

        @pl.when(relay.at(r, h))
        def _():
            for m, o, src, dst in mats:

                @pl.when(d == o)
                def _():
                    pltpu.make_async_copy(src, dst.at[d], own.at[0]).start()

                @pl.when(d != o)
                def _():
                    remote(src, dst.at[d], send.at[m], recv.at[d], dev(o, s)).start()

    for (r, h), items in shared.items():

        @pl.when(relay.at(1 - r, h))
        def _():
            for i, src, dst in items:
                relay.middle(i, dst)

    for r, h, mats in groups:

        @pl.when(relay.at(r, h))
        def _():
            for i, src, dst in shared[(r, h)]:
                pltpu.make_async_copy(src, dst, gown.at[i]).wait()
            for m, o, src, dst in mats:

                @pl.when(d == o)
                def _():
                    pltpu.make_async_copy(src, dst.at[d], own.at[0]).wait()

                    def arrived(k, carry):
                        p = lax.rem(d + n - k, n)
                        remote(src, dst.at[p], send.at[m], recv.at[p], dev(p, s)).wait_recv()
                        return carry

                    lax.fori_loop(1, n, arrived, 0)

                @pl.when(d != o)
                def _():
                    remote(src, dst.at[d], send.at[m], recv.at[d], dev(o, s)).wait_send()

    for (r, h), items in shared.items():
        relay.finish(r, h, items)


def spread_kernel(n, xa, xf, gy1, summed, oa, of, xy1, xy2, send, recv, rsend, rrecv, own, gown):
    relay = Relay(rsend, rrecv)
    d, s, role, half = relay.d, relay.s, relay.role, relay.half
    greet_dp(n, [relay.other, relay.mate])
    groups = []
    for r in range(2):
        mats = 4 if r == 0 else 8
        groups.append((r, 0, mats, functools.partial(owner_first, r), xa, oa, 10 * r, 4))
        groups.append((r, 1, 2, owner_second, xf, of, 10 * r + 8, 2))
    text = {
        (0, 0): [(20, gy1, xy1.at[0])],
        (0, 1): [(21, gy1, xy1.at[1])],
        (1, 1): [(22, summed.at[8], xy2)],
    }
    for (r, h), items in text.items():

        @pl.when(relay.at(r, h))
        def _():
            for i, src, dst in items:
                pltpu.make_async_copy(src, dst, gown.at[i - 20]).start()
                relay.start(i, src, dst)

    for r, h, mats, owner, src, dst, base, per in groups:

        @pl.when(relay.at(r, h))
        def _():
            for m in range(mats):

                @pl.when(d == owner(m))
                def _():
                    pltpu.make_async_copy(src.at[d], dst.at[per * r + m], own.at[m]).start()

                    def start(k, carry):
                        to = lax.rem(d + k, n)
                        remote(
                            src.at[to], dst.at[per * r + m], send.at[k], recv.at[m], dev(to, s)
                        ).start()
                        return carry

                    lax.fori_loop(1, n, start, 0)

            for m in range(mats):

                @pl.when(d == owner(m))
                def _():
                    pltpu.make_async_copy(src.at[d], dst.at[per * r + m], own.at[m]).wait()

                @pl.when(d != owner(m))
                def _():
                    remote(
                        src.at[d], dst.at[per * r + m], send.at[1], recv.at[m], dev(owner(m), s)
                    ).wait_recv()

                relay.start(base + m, dst.at[per * r + m], dst.at[per * r + m])

    for (r, h), items in text.items():

        @pl.when(relay.at(1 - r, h))
        def _():
            for i, src, dst in items:
                relay.middle(i, dst)

    for r, h, mats, owner, src, dst, base, per in groups:

        @pl.when(relay.at(1 - r, h))
        def _():
            for m in range(mats):
                relay.middle(base + m, dst.at[per * r + m])

    for r, h, mats, owner, src, dst, base, per in groups:

        @pl.when(relay.at(r, h))
        def _():
            for m in range(mats):

                @pl.when(d == owner(m))
                def _():
                    def finish(k, carry):
                        to = lax.rem(d + k, n)
                        remote(
                            src.at[to], dst.at[per * r + m], send.at[k], recv.at[m], dev(to, s)
                        ).wait_send()
                        return carry

                    lax.fori_loop(1, n, finish, 0)

        relay.finish(r, h, [(base + m, dst.at[per * r + m], dst.at[per * r + m]) for m in range(mats)])

    for (r, h), items in text.items():

        @pl.when(relay.at(r, h))
        def _():
            for i, src, dst in items:
                pltpu.make_async_copy(src, dst, gown.at[i - 20]).wait()

        relay.finish(r, h, items)


def adamw_update(weight, first, second, grad, fix_one, fix_two):
    first = beta_one * first + (1.0 - beta_one) * grad
    second = beta_two * second + (1.0 - beta_two) * grad * grad
    first_hat = first / fix_one
    second_hat = second / fix_two
    weight = weight - adam_rate * (
        first_hat / (jnp.sqrt(second_hat) + 1e-08) + weight_decay * weight
    )
    return (weight, first, second)


def update_kernel(
    rates, pieces, scal, stat,
    aw, am, ag, ax, fw, fm, fg, fx, sw, s1, s2, gv, g1, g2, gt, gy2, gm, vw, v1, v2, gvall, gtall,
    aw_, am_, ab_, fw_, fm_, fb_, sw_, s1_, s2_, sb_, vw_, v1_, v2_, vb_, loss_, norm_,
):
    grad_norm = jnp.sqrt(stat[0:1, 0:1])
    factor = jnp.minimum(1.0, max_norm / (grad_norm + 1e-06))
    fix_one, fix_two = scal[0], scal[1]
    loss_[...] = stat[4:5, 0:1]
    norm_[...] = grad_norm
    shrink = 1.0 - muon_rate * weight_decay
    for rate, (w, m, g, x, w_, m_, b_) in zip(
        rates, ((aw, am, ag, ax, aw_, am_, ab_), (fw, fm, fg, fx, fw_, fm_, fb_))
    ):
        m_[...] = momentum_decay * m[...] + g[...] * factor
        fresh = w[...] * shrink - rate * x[...].astype(f32)
        w_[...] = fresh
        b_[...] = low(fresh)
    text = gt.shape[1] - 128
    shards = {
        "embed": gv[:, EMB0 : EMB0 + 16],
        "time": g1[...],
        "time2": g2[...],
        "text": None,
        "text2": gy2[...],
        "head": gv[:, HEAD0 : HEAD0 + 16],
        "mod": gm[...],
    }
    for name, at, size in pieces:
        stride = size if name != "text" else 512
        for start in range(0, size, stride):
            cut = slice(at + start, at + start + stride)
            grad = gt[:, start : start + stride].astype(f32) if name == "text" else shards[name]
            fresh, one, two = adamw_update(
                sw[:, cut], s1[:, cut], s2[:, cut], grad * factor, fix_one, fix_two
            )
            sw_[:, cut], s1_[:, cut], s2_[:, cut] = fresh, one, two
            sb_[:, cut] = low(fresh)

    @pl.when(pl.program_id(0) == 0)
    def _():
        lane = lax.broadcasted_iota(jnp.int32, (1, 128), 1)
        column = gtall[:, text : text + 128].astype(f32)
        whole = jnp.where(lane == 9, column, gvall[...])
        rows = vw.shape[0]
        grad = jnp.transpose(whole)[0:rows, :] * factor
        fresh, one, two = adamw_update(vw[...], v1[...], v2[...], grad, fix_one, fix_two)
        vw_[...], v1_[...], v2_[...] = fresh, one, two
        vb_[...] = low(fresh)


def body(
    latents,
    noise_draw,
    timesteps,
    captions,
    caption_len,
    attention_weights,
    feed_weights,
    side_weights,
    vector_weights,
    attention_momentum,
    feed_momentum,
    side_first,
    side_second,
    vector_first,
    vector_second,
    step_count,
):
    n = lax.axis_size("dp")
    d, s = here()
    role, half = s // 2, lax.rem(s, 2)
    count = latents.shape[0]
    frames = latents.shape[1]
    width = attention_weights.shape[1]
    cols, feed_cols = attention_weights.shape[2], feed_weights.shape[2]
    hidden = n * feed_cols
    text = captions.shape[2]
    sds = jax.ShapeDtypeStruct
    role_s, half_s = role.reshape(1).astype(jnp.int32), half.reshape(1).astype(jnp.int32)

    o_time = 16
    o_text = o_time + 256 + width
    o_text2 = o_text + text
    o_head = o_text2 + width
    o_mod = o_head + 16
    six = 6 * width
    own_rows = -(-cols // 2)
    lanes = n * own_rows

    att_t = jnp.swapaxes(attention_weights, 1, 2)
    feed_t = jnp.swapaxes(feed_weights, 1, 2)
    side_t = side_weights.T
    pa, pb, pf, pw, py, pm, wm_own = local_call(
        lambda role, half, *refs: pack_kernel(
            role, half, (o_time, o_text, o_text2, o_head, o_mod), *refs
        ),
        [
            sds((4, cols, width), bf16),
            sds((4, cols, width), bf16),
            sds((2, feed_cols, width), bf16),
            sds((cols, 1152), bf16),
            sds((own_rows, text), bf16),
            sds((cols, 3 * width), bf16),
            sds((cols, six), bf16),
        ],
        [SM] * 2 + [VM] * 4,
        (role_s, half_s, att_t, feed_t, side_t, vector_weights.T),
    )
    freqs = jnp.exp(-math.log(10000.0) * jnp.arange(128, dtype=f32) / 128)
    angles = timesteps.astype(f32)[:, None] * freqs[None, :]
    level, snr = snr_weight(timesteps.astype(f32))
    pt = jnp.concatenate([jnp.cos(angles), jnp.sin(angles), snr[:, None]], axis=1)
    pt = jnp.pad(pt, ((0, 8 - count), (0, width - 257)))

    wa, wb, wf, ww, wy, wm, wt = comm_call(
        functools.partial(gather_kernel, n),
        1,
        (pa, pb, pf, pw, py, pm, pt),
        [
            sds((4, n, cols, width), bf16),
            sds((4, n, cols, width), bf16),
            sds((2, n, feed_cols, width), bf16),
            sds((n, cols, 1152), bf16),
            sds((n, own_rows, text), bf16),
            sds((n, cols, 3 * width), bf16),
            sds((n, 8, width), f32),
        ],
        [(4, 7, n), (7, n), (7, n), (7,)],
    )
    wa = wa.reshape(4, width, width)
    wb = wb.reshape(4, width, width)
    wf = wf.reshape(2, hidden, width)
    ww = ww.reshape(width, 1152)
    wy = wy.reshape(lanes, text)
    wm = wm.reshape(width, 3 * width)
    rank_s = d.reshape(1).astype(jnp.int32)
    per_clip = frames * (latents.shape[3] // 2) * (latents.shape[4] // 2)
    vec, hid, temb, mq_own, y2p, errs = local_call(
        functools.partial(condition_kernel, per_clip=per_clip, cols=cols),
        [
            sds((128, width), f32),
            sds((n * 8, width), f32),
            sds((n * 8, width), f32),
            sds((8, 3 * width), f32),
            sds((2, width, lanes), bf16),
            sds((8, 128), f32),
        ],
        [SM] + [VM] * 3,
        (rank_s, wt.reshape(n * 8, width), ww, wm),
    )
    mq = comm_call(
        mate_kernel, 2, (mq_own,), sds((2, 8, 3 * width), f32), [(1,), (1,), (1,)]
    )

    half_tokens = count * per_clip // 2

    def own_rows_of(value):
        return lax.dynamic_slice_in_dim(
            value.reshape(count * per_clip, 16), half * half_tokens, half_tokens, 0
        )

    def tokens(clean, noise):
        mix = level[:, None, None, None, None]
        noisy = low(jnp.sqrt(mix) * clean + jnp.sqrt(1.0 - mix) * noise)
        return jnp.pad(own_rows_of(patchify(noisy)), ((0, 0), (EMB0, 112 - EMB0)))

    def targets(noise):
        value = patchify(noise).reshape(count, frames, 2, 32, 16).transpose(0, 2, 1, 3, 4)
        return jnp.pad(own_rows_of(value), ((0, 0), (HEAD0, 112 - HEAD0)))

    tok = lax.cond(
        role == 0,
        tokens,
        lambda clean, noise: jnp.zeros((half_tokens, 128), bf16),
        latents,
        noise_draw,
    )
    places = np.arange(per_clip // frames)
    edge = latents.shape[3] // 2
    pos = np.concatenate(
        [sincos(places // edge, width // 2), sincos(places % edge, width // 2)], axis=1
    )
    pos = jnp.asarray(pos)
    timing = jnp.asarray(sincos(np.arange(frames), width))

    clip_rows = captions.shape[1]
    residuals = [
        sds((5, half_tokens, width), bf16),
        sds((3, half_tokens, width), f32),
        sds((half_tokens, hidden), f32),
        sds((count, 3, 256, 128), f32),
    ]
    residual_scratch = [pltpu.VMEM(v.shape, v.dtype) for v in residuals]
    h1s, hq, gq_own, kept_b, kept_f, kept_u, kept_p = local_call(
        functools.partial(first_kernel, cols),
        [
            sds((count, 2, 64, width), bf16),
            sds((count, LP, lanes), f32),
            sds((count, LP, lanes), bf16),
        ]
        + residuals,
        [SM] * 2 + [VM] * 7 + [ANY],
        (role_s, half_s, tok, pos, mq, vec, wa, wf, wy, captions),
        residual_scratch
        + [
            pltpu.VMEM((count, clip_rows, text), bf16),
            pltpu.SemaphoreType.DMA((count,)),
            pltpu.SemaphoreType.DMA((count, 4)),
        ],
        [VM] * 3 + [ANY] * 4,
    )
    later_noise, gq_own = lax.optimization_barrier((noise_draw, gq_own))
    target = lax.cond(
        role == 1,
        targets,
        lambda noise: jnp.zeros((half_tokens, 128), f32),
        later_noise,
    )
    target, h1s = lax.optimization_barrier((target, h1s))
    h1t, rgq, mqt = comm_call(
        functools.partial(forward_kernel, count),
        3,
        (h1s, gq_own, mq),
        [
            sds((count, 2, 64, width), bf16),
            sds((count, LP, lanes), bf16),
            sds((2, 8, 3 * width), f32),
        ],
        [(count, 2), (count, 2), (1,), (1,), (2,), (2,)],
    )

    ncl = (count + 1) // 2
    wide = sds((2, half_tokens, hidden), bf16)
    thin = sds((2, half_tokens, width), bf16)
    cap_like = sds((ncl, LP, width), bf16)
    dh1, acts_t, actf_t, actw_t, ybuf, dkv, grads_t, dmod_t, loss_t = local_call(
        temporal_kernel,
        [
            sds((count, 2, 64, width), bf16),
            sds((10, half_tokens, width), bf16),
            thin,
            wide,
            cap_like,
            sds((2, ncl, LP, width), f32),
            sds((128, width), f32),
            sds((count, 8, width), f32),
            sds((1, 128), f32),
        ],
        [SM] * 4 + [VM] * 13,
        (
            role_s, half_s, rank_s, caption_len, errs, h1t, timing, mqt, vec, temb, wa, wb, wf,
            gq_own, rgq, y2p, target,
        ),
        [pltpu.VMEM((ncl, KP, width), bf16), pltpu.VMEM((ncl, KP, width), bf16)],
    )
    dhs, extra, dmods_t = comm_call(
        functools.partial(backward_kernel, count),
        4,
        (dh1, dkv, dmod_t),
        [
            sds((count, 2, 64, width), bf16),
            sds((2, LP, width), f32),
            sds((2, count, 8, width), f32),
        ],
        [(count, 2), (count, 2), (1,), (1,), (2,), (2,)],
    )
    acts_s, actf_s, actw_s, dkvb, dy, vect, dmod = local_call(
        last_kernel,
        [
            sds((6, half_tokens, width), bf16),
            thin,
            wide,
            sds((2, ncl, LP, width), bf16),
            cap_like,
            sds((width, 128), f32),
            sds((count, 8, width), f32),
        ],
        [SM] * 2 + [VM] * 6 + [ANY] * 4 + [VM] * 5,
        (
            role_s, half_s, tok, mq, vec, wa, wb, wf, kept_b, kept_f, kept_u, kept_p, dhs, dkv,
            extra, grads_t, dmod_t,
        ),
        [pltpu.VMEM((128, width), f32)]
        + residual_scratch
        + [pltpu.SemaphoreType.DMA((count, 4))],
    )
    racts, ractf, ractw, rybuf, rdkvb, rdy, rdmod = comm_call(
        swap_kernel,
        5,
        (acts_s, acts_t, actf_s, actf_t, actw_s, actw_t, ybuf, dkvb, dy, dmod),
        [
            sds((10, half_tokens, width), bf16),
            thin,
            wide,
            cap_like,
            sds((2, ncl, LP, width), bf16),
            cap_like,
            sds((count, 8, width), f32),
        ],
        [(5,), (5,)],
    )
    line = n // 2
    wide_text = text + 128
    cut_text = wide_text // TEXT_CUTS
    block = (9, line, cols, width)
    tokens2 = 2 * half_tokens
    grad_own, grad_snd, text_part = local_call(
        weight_grad_kernel,
        [
            sds(block, f32),
            sds(block, bf16),
            sds((line, 2, own_rows, wide_text), bf16),
        ],
        [SM] * 3 + [ANY] * 9 + [VM] * 10 + [ANY],
        (
            role_s, half_s, rank_s, acts_s, acts_t, racts, actf_s, actf_t, ractf, actw_s, actw_t,
            ractw, ybuf, rybuf, dkvb, rdkvb, dy, rdy, gq_own, rgq, hq, y2p, captions,
        ),
        [
            pltpu.VMEM((10, tokens2, width), bf16),
            pltpu.VMEM((2, tokens2, width), bf16),
            pltpu.VMEM((2, tokens2, hidden), bf16),
            pltpu.VMEM((count, clip_rows, text), bf16),
            pltpu.VMEM((width, width), f32),
            pltpu.VMEM((count, lanes, LP), bf16),
            pltpu.VMEM((lanes, 128), f32),
            pltpu.SemaphoreType.DMA((4 + count,)),
        ],
    )

    mine0 = jnp.where(half == 0, dmod, rdmod)
    mine1 = jnp.where(half == 0, rdmod, dmod)
    sources = (mine0, mine1, dmods_t[0], dmods_t[1])
    dm_clip = []
    for clip in range(count):
        total = 0.0
        for seg in range(4):
            for i in range(count):
                if ((seg % 2) * count + i) // 2 == clip:
                    total = total + sources[seg][i]
        dm_clip.append(total)
    dm = jnp.concatenate(dm_clip, axis=0)

    whole_clips = n * 8
    text_block = (TEXT_CUTS, line, own_rows, cut_text)
    summed, text_sum, vsum, tile, grad_mod, grad_time2, grad_time1 = comm_call(
        functools.partial(scatter_kernel, n),
        6,
        (
            grad_own, grad_snd, text_part, dm, vect.reshape(n, cols, 128), loss_t,
            wm_own, temb, ww, hid, wt.reshape(whole_clips, width),
        ),
        [
            sds((9, cols, width), f32),
            sds((own_rows, wide_text), bf16),
            sds((cols, 128), f32),
            sds((8, width), f32),
            sds((cols, six), f32),
            sds((cols, width), f32),
            sds((cols, 256), f32),
        ],
        [(9,), (9 + TEXT_CUTS,), (9 + TEXT_CUTS,)]
        + [(TEXT_CUTS + 1, line)] * 2
        + [(8, line)] * 4
        + [(2, n), (2, n), (2,), (TEXT_CUTS,), (TEXT_CUTS,), (n,), (n,)],
        [VM] * 7,
        in_specs=[ANY] * 5 + [VM] * 6,
        scratch=[
            pltpu.VMEM(block, f32),
            pltpu.VMEM(block, bf16),
            pltpu.VMEM((8,) + block[1:], f32),
            pltpu.VMEM((8,) + block[1:], f32),
            pltpu.VMEM(block[1:], bf16),
            pltpu.VMEM(block[1:], bf16),
            pltpu.VMEM((TEXT_CUTS, line, 2, own_rows, cut_text), bf16),
        ]
        + [pltpu.VMEM(text_block, bf16)] * 3
        + [
            pltpu.VMEM((n, cols, 128), f32),
            pltpu.VMEM((n * 8 * count, width), f32),
            pltpu.VMEM((n, whole_clips, 128), f32),
        ],
    )

    att_m = jnp.swapaxes(attention_momentum, 1, 2)
    feed_m = jnp.swapaxes(feed_momentum, 1, 2)
    ua, uf, ga2, gf2, grad_mod, grad_time2, grad_time1, grad_v, stat = comm_call(
        functools.partial(settle_kernel, n),
        8,
        (
            vsum, tile, summed, att_m, feed_m.reshape(16, cols, width), grad_mod, grad_time2,
            grad_time1,
        ),
        [
            sds((n, cols, width), f32),
            sds((n, 4, cols, width), f32),
            sds((12, cols, width), f32),
            sds((16, cols, width), f32),
            sds((cols, six), f32),
            sds((cols, width), f32),
            sds((cols, 256), f32),
            sds((cols, 128), f32),
            sds((8, 128), f32),
        ],
        [(1,), (8,), (n,), (1,), (7, 3), (7, 3), (7,), (2, 4), (2, 4), (n,), (n,)],
        [ANY] * 7 + [VM] * 2,
        in_specs=[VM] * 3 + [ANY] * 5,
        scratch=[
            pltpu.VMEM((4, cols, 128), f32),
            pltpu.VMEM((4, 8, width), f32),
            pltpu.VMEM((8, 128), f32),
            pltpu.VMEM((n, 8, 128), f32),
            pltpu.VMEM((8, cols, width), f32),
            pltpu.VMEM((8, cols, width), f32),
        ],
    )
    xa, xf = local_call(
        muon_kernel,
        [sds((width, width), bf16), sds((hidden, width), bf16)],
        [SM] + [VM] * 2,
        (half_s, ua.reshape(width, width), uf.reshape(hidden, width)),
        [pltpu.VMEM((width, width), f32), pltpu.VMEM((width, width), f32)],
    )
    xa_all, xf_all, gy12, gy22 = comm_call(
        functools.partial(spread_kernel, n),
        10,
        (xa.reshape(n, cols, width), xf.reshape(n, feed_cols, width), text_sum, summed),
        [
            sds((12, cols, width), bf16),
            sds((4, feed_cols, width), bf16),
            sds((2, own_rows, wide_text), bf16),
            sds((cols, width), f32),
        ],
        [(n,), (8,), (23, 3), (23, 3), (8,), (3,)],
    )

    clock = step_count[0].astype(f32)
    scal = jnp.stack([1.0 - jnp.power(beta_one, clock), 1.0 - jnp.power(beta_two, clock)])
    text_grad = gy12.reshape(2 * own_rows, wide_text)[:cols]
    side_m, side_v = side_first.T, side_second.T
    side_rows = side_t.shape[1]
    pieces = (
        ("embed", 0, 16),
        ("time", o_time, 256),
        ("time2", o_time + 256, width),
        ("text", o_text, text),
        ("text2", o_text2, width),
        ("head", o_head, 16),
        ("mod", o_mod, six),
    )
    rates = tuple(
        muon_rate * 0.2 * math.sqrt(columns) for columns in (n * cols, n * feed_cols)
    )
    grid = cols // 8 if cols % 8 == 0 else 1

    def by_rows(value):
        return value.reshape(-1, value.shape[-1])

    def rows_spec(value):
        return pl.BlockSpec((value.shape[0] // grid, value.shape[1]), lambda i: (i, 0))

    def whole_spec(value):
        return pl.BlockSpec(value.shape, lambda i: (0, 0))

    cutup = [by_rows(v) for v in (att_t, att_m, ga2, xa_all, feed_t, feed_m, gf2, xf_all)] + [
        side_t, side_m, side_v, grad_v, grad_time1, grad_time2, text_grad, gy22, grad_mod,
    ]
    fixed = [vector_weights, vector_first, vector_second, grad_v, text_grad]
    a_like, f_like, s_like = (sds(v.shape, f32) for v in (cutup[0], cutup[4], side_t))
    v_like = sds(vector_weights.shape, f32)

    def low_of(like):
        return sds(like.shape, bf16)

    row_outs = [
        a_like, a_like, low_of(a_like), f_like, f_like, low_of(f_like), s_like, s_like, s_like,
        low_of(s_like),
    ]
    whole_outs = [v_like, v_like, v_like, low_of(v_like), sds((1, 1), f32), sds((1, 1), f32)]
    (
        att_new, att_moment, att_low, feed_new, feed_moment, feed_low, side_new, side_first_new,
        side_second_new, side_low, vector_new, vector_first_new, vector_second_new, vector_low,
        loss_value, grad_norm,
    ) = pl.pallas_call(
        functools.partial(update_kernel, rates, pieces),
        grid=(grid,),
        out_shape=row_outs + whole_outs,
        in_specs=[SM, whole_spec(stat)] + [rows_spec(v) for v in cutup] + [whole_spec(v) for v in fixed],
        out_specs=[rows_spec(v) for v in row_outs] + [whole_spec(v) for v in whole_outs],
        compiler_params=pltpu.CompilerParams(vmem_limit_bytes=VMEM_LIMIT),
    )(scal, stat, *cutup, *fixed)

    def att(value):
        return value.reshape(att_t.shape)

    def feed(value):
        return value.reshape(feed_t.shape)

    def back(value):
        return jnp.swapaxes(value, -1, -2)

    return (
        loss_value[0, 0],
        grad_norm[0, 0],
        back(att(att_new)),
        back(att(att_moment)),
        back(feed(feed_new)),
        back(feed(feed_moment)),
        back(side_new),
        back(side_first_new),
        back(side_second_new),
        vector_new,
        vector_first_new,
        vector_second_new,
        back(att(att_low)),
        back(feed(feed_low)),
        back(side_low),
        vector_low,
    )


def solution(mesh):
    column = P(None, "dp")
    matrix = P(None, None, "dp")
    return jax.shard_map(
        body,
        mesh=mesh,
        in_specs=(
            P("dp", None, None, None, None),
            P("dp", None, None, None, None),
            P("dp"),
            P("dp", None, None),
            P("dp"),
            matrix,
            matrix,
            column,
            column,
            matrix,
            matrix,
            column,
            column,
            column,
            column,
            P(),
        ),
        out_specs=(
            P(),
            P(),
            matrix,
            matrix,
            matrix,
            matrix,
            column,
            column,
            column,
            column,
            column,
            column,
            matrix,
            matrix,
            column,
            column,
        ),
        check_vma=False,
    )
```

profile of v0, /device:TPU:27, one launch (start us, length us, event | category | flops | bytes accessed | tf_op | source)
XLA Modules:
  0.0 320.6 jit_solution(2412859491593285058)
XLA Ops:
  0.7 1.4 copy.52
  2.1 3.4 %shard_map.298 = (bf16[4,48,384]{2,1,0:T(8,128)(2,1)}, bf16[4,48,384]{2,1,0:T(8,128)(2,1)}, bf16[2,192,384]{2,1,0:T(8,128)(2,1)}, bf16[48,1152]{1,0:T(8,128)(2,1...) custom-call(s32[1]{0:T(128)} %bitcast.7.role, s32[1]{0:T(128)} %bitcast.8.half, ...), custom_call_target="tpu_custom_call" | custom-call | tf_op jit(solution)/shard_map/pallas_call | solution.py:784
  5.5 0.1 multiply_cosine_fusion
  5.7 0.1 copy.53
  5.8 0.6 select_maximum_fusion.pt
  6.4 40.6 %shard_map.299 = (bf16[4,8,48,384]{3,2,1,0:T(8,128)(2,1)}, bf16[4,8,48,384]{3,2,1,0:T(8,128)(2,1)}, bf16[2,8,192,384]{3,2,1,0:T(8,128)(2,1)}, bf16[8,48,1152]{2,...) custom-call(bf16[4,48,384]{2,1,0:T(8,128)(2,1)} %get-tuple-element.141.pa, ...), custom_call_target="tpu_custom_call" | custom-call | tf_op jit(solution)/shard_map/pallas_call | solution.py:835
  47.0 3.1 shard_map.300
  50.1 2.6 shard_map.301.mq
  52.7 8.9 %conditional.2 = (bf16[384,128]{1,0:T(8,128)(2,1)}) conditional(s32[]{:T(128)} %convert_element_type.24, () %tuple.22, (f32[3]{0:T(128)S(1)}, f32[3,4,4,16,16]{4,3,2,1,0:T(8,128)S(1)}, f32[3,4,4,16,16]{4,3,2,1,0:T(8,128)S(1)}, s32[]{:T(128)}) %tuple.47), branch_computations={%region_0.1_spmd, %region_1.2_spmd} | conditional | flops 49159 | bytes 577656 | solution.py:2052
  52.7 1.2 copy.50
  53.9 1.2 copy.51
  55.1 1.2 add_convert_fusion
  56.3 3.9 %copy.47 = bf16[3,4,8,8,2,2,4]{3,2,1,0,6,5,4:T(8,128)(2,1)S(1)} copy(bf16[3,4,8,8,2,2,4]{6,5,3,4,2,1,0:T(2,128)(2,1)} %bitcast.132) | data formatting | bytes 49152 | tf_op jit(solution)/shard_map/cond/branch_1_fun/transpose | solution.py:63
  60.2 0.5 reshape.143
  60.7 0.1 copy.60
  60.9 0.7 pad.9.clone
  61.6 11.9 %shard_map.302 = (bf16[3,2,64,384]{3,2,1,0:T(8,128)(2,1)}, f32[3,304,192]{2,1,0:T(8,128)}, bf16[3,304,192]{2,1,0:T(8,128)(2,1)}, bf16[5,384,384]{2,1,0:T(8,128)(...) custom-call(s32[1]{0:T(128)} %bitcast.7.role, s32[1]{0:T(128)} %bitcast.8.half, ...), custom_call_target="tpu_custom_call" | custom-call | tf_op jit(solution)/shard_map/pallas_call | solution.py:784
  73.5 14.2 %shard_map.303 = (bf16[3,2,64,384]{3,2,1,0:T(8,128)(2,1)}, bf16[3,304,192]{2,1,0:T(8,128)(2,1)}, f32[2,8,1152]{2,1,0:T(8,128)}) custom-call(bf16[3,2,64,384]{3,2,1,0:T(8,128)(2,1)} %get-tuple-element.164.h1s, bf16[3,304,192]{2,1,0:T(8,128)(2,1)} %get-tuple-element.165.gq, f32[2,8,1152]{2,1,0:T(8,128)} %shard_map.301.mq), custom_call_target="tpu_custom_call" | custom-call | tf_op jit(solution)/shard_map/pallas_call | solution.py:835
  87.8 0.8 copy.56.target
  88.6 6.6 %shard_map.304 = (bf16[3,2,64,384]{3,2,1,0:T(8,128)(2,1)}, bf16[10,384,384]{2,1,0:T(8,128)(2,1)}, bf16[2,384,384]{2,1,0:T(8,128)(2,1)}, bf16[2,384,1536]{2,1,0:T...) custom-call(s32[1]{0:T(128)} %bitcast.7.role, ...), custom_call_target="tpu_custom_call" | custom-call | tf_op jit(solution)/shard_map/pallas_call | solution.py:784
  95.2 38.1 %shard_map.305 = (bf16[3,2,64,384]{3,2,1,0:T(8,128)(2,1)}, f32[2,304,384]{2,1,0:T(8,128)}, f32[2,3,8,384]{3,2,1,0:T(8,128)}) custom-call(bf16[3,2,64,384]{3,2,1,0:T(8,128)(2,1)} %get-tuple-element.172.dh1, f32[2,2,304,384]{3,2,1,0:T(8,128)} %get-tuple-element.173.dkv, f32[3,8,384]{2,1,0:T(8,128)} %get-tuple-element.174.dmod.dmod_t), custom_call_target="tpu_custom_call" | custom-call | tf_op jit(solution)/shard_map/pallas_call | solution.py:835
  133.2 16.4 %shard_map.306 = (bf16[6,384,384]{2,1,0:T(8,128)(2,1)}, bf16[2,384,384]{2,1,0:T(8,128)(2,1)}, bf16[2,384,1536]{2,1,0:T(8,128)(2,1)}, bf16[2,2,304,384]{3,2,1,0:T...) custom-call(s32[1]{0:T(128)} %bitcast.7.role, s32[1]{0:T(128)} %bitcast.8.half, ...), custom_call_target="tpu_custom_call" | custom-call | tf_op jit(solution)/shard_map/pallas_call | solution.py:784
  149.6 5.9 %shard_map.307 = (bf16[10,384,384]{2,1,0:T(8,128)(2,1)}, bf16[2,384,384]{2,1,0:T(8,128)(2,1)}, bf16[2,384,1536]{2,1,0:T(8,128)(2,1)}, bf16[2,304,384]{2,1,0:T(8,...) custom-call(bf16[6,384,384]{2,1,0:T(8,128)(2,1)} %get-tuple-element.178.acts_s, ...), custom_call_target="tpu_custom_call" | custom-call | tf_op jit(solution)/shard_map/pallas_call | solution.py:835
  155.6 0.8 broadcast_select_fusion.1
  156.4 0.6 pad_maximum_fusion.dm
  157.0 12.3 %shard_map.308 = (f32[9,4,48,384]{3,2,1,0:T(8,128)}, bf16[9,4,48,384]{3,2,1,0:T(8,128)(2,1)}, bf16[4,2,24,4224]{3,2,1,0:T(8,128)(2,1)}) custom-call(s32[1]{0:T(128)} %bitcast.7.role, s32[1]{0:T(128)} %bitcast.8.half, s32[1]{0:T(128)} %bitcast.9.rank, bf16[6,384,384]{2,1,0:T(8,128)(2,1)} %get-tuple-element.178.acts_s, ...), custom_call_target="tpu_custom_call" | custom-call | tf_op jit(solution)/shard_map/pallas_call | solution.py:784
  169.3 70.2 %shard_map.309 = (f32[9,48,384]{2,1,0:T(8,128)}, bf16[24,4224]{1,0:T(8,128)(2,1)}, f32[48,128]{1,0:T(8,128)}, f32[8,384]{1,0:T(8,128)}, f32[48,2304]{1,0:T(8,128...) custom-call(f32[9,4,48,384]{3,2,1,0:T(8,128)} %get-tuple-element.195.own_in, bf16[9,4,48,384]{3,2,1,0:T(8,128)(2,1)} %get-tuple-element.196.snd, ...), custom_call_target="tpu_custom_call" | custom-call | tf_op jit(solution)/shard_map/pallas_call | solution.py:835
  239.5 21.9 %shard_map.310 = (f32[8,48,384]{2,1,0:T(8,128)}, f32[8,4,48,384]{3,2,1,0:T(8,128)}, f32[12,48,384]{2,1,0:T(8,128)}, f32[16,48,384]{2,1,0:T(8,128)}, f32[48,2304]...) custom-call(f32[48,128]{1,0:T(8,128)} %get-tuple-element.204.vsum, ...), custom_call_target="tpu_custom_call" | custom-call | tf_op jit(solution)/shard_map/pallas_call | solution.py:835
  261.4 19.8 %shard_map.311 = (bf16[384,384]{1,0:T(8,128)(2,1)}, bf16[1536,384]{1,0:T(8,128)(2,1)}) custom-call(s32[1]{0:T(128)} %bitcast.8.half, f32[384,384]{1,0:T(8,128)} %bitcast.144, f32[1536,384]{1,0:T(8,128)} %bitcast.133), custom_call_target="tpu_custom_call" | custom-call | tf_op jit(solution)/shard_map/pallas_call | solution.py:784
  281.2 26.7 %shard_map.312 = (bf16[12,48,384]{2,1,0:T(8,128)(2,1)}, bf16[4,192,384]{2,1,0:T(8,128)(2,1)}, bf16[2,24,4224]{2,1,0:T(8,128)(2,1)}, f32[48,384]{1,0:T(8,128)}) custom-call(bf16[8,48,384]{2,1,0:T(8,128)(2,1)} %bitcast.149, bf16[8,192,384]{2,1,0:T(8,128)(2,1)} %bitcast.139, bf16[24,4224]{1,0:T(8,128)(2,1)} %get-tuple-element.216.gy1, ...), custom_call_target="tpu_custom_call" | custom-call | tf_op jit(solution)/shard_map/pallas_call | solution.py:835
  308.6 0.6 pad_maximum_fusion.1.scal
  309.2 11.2 %shard_map.313 = (f32[576,384]{1,0:T(8,128)}, f32[576,384]{1,0:T(8,128)}, bf16[576,384]{1,0:T(8,128)(2,1)}, f32[768,384]{1,0:T(8,128)}, f32[768,384]{1,0:T(8,128...) custom-call(f32[2]{0:T(128)} %pad_maximum_fusion.1.scal, ...), custom_call_target="tpu_custom_call" | custom-call | tf_op jit(solution)/shard_map/pallas_call | solution.py:2365
  (18 shorter events, 0.2 us)
Async XLA Ops:
  2.1 3.4 %copy-start.4 = (s32[3]{0:T(128)S(1)}, s32[3]{0:T(128)}, u32[]{:S(2)}) copy-start(s32[3]{0:T(128)} %param.24) | copy-start | bytes 40
  5.5 47.2 %copy-start = (f32[3,4,4,16,16]{4,3,2,1,0:T(8,128)S(1)}, f32[3,4,4,16,16]{4,3,2,1,0:T(8,128)}, u32[]{:S(2)}) copy-start(f32[3,4,4,16,16]{4,3,2,1,0:T(8,128)} %param.23) | copy-start | bytes 147460
  5.5 47.2 %copy-start.1 = (f32[3,4,4,16,16]{4,3,2,1,0:T(8,128)S(1)}, f32[3,4,4,16,16]{4,3,2,1,0:T(8,128)}, u32[]{:S(2)}) copy-start(f32[3,4,4,16,16]{4,3,2,1,0:T(8,128)} %param.22) | copy-start | bytes 147460
  149.6 5.9 %copy-start.2 = (f32[3,8,384]{2,1,0:T(8,128)S(1)}, f32[3,8,384]{2,1,0:T(8,128)}, u32[]{:S(2)}) copy-start(f32[3,8,384]{2,1,0:T(8,128)} %get-tuple-element.187.dmod) | copy-start | bytes 110596
  149.6 6.7 %copy-start.3 = (f32[2,3,8,384]{3,2,1,0:T(8,128)S(1)}, f32[2,3,8,384]{3,2,1,0:T(8,128)}, u32[]{:S(2)}) copy-start(f32[2,3,8,384]{3,2,1,0:T(8,128)} %get-tuple-element.199) | copy-start | bytes 221188
where the time goes:
time: 323 us; the launch traced here: 321 us
  Pallas kernels  305 us (94%)
  local copies, waits for them, and re-layouts  10 us (3%)
  other arithmetic  3.96 us (1%)
    pallas_call x8, Pallas kernels, comm_call(): pl.pallas_call(kernel, out_shape=out_shape, in_specs=[ANY] * len(args) if...  220 us
    pallas_call x7, Pallas kernels, local_call(): pl.pallas_call(kernel, out_shape=out_shape, in_specs=in_specs, out_specs=...  73.4 us
    pallas_call x1, Pallas kernels, body(): pl.pallas_call(functools.partial(update_kernel, rates, pieces), grid=(gri...  11.2 us

commit v1 on v0

--- a/solution.py
+++ b/solution.py
@@ -232,7 +232,7 @@
     pw[:, first : first + width] = rounded(text2, width)
     cols = pw.shape[0]
     pw[:, first + width :] = low(jnp.concatenate(
-        [vec[...], side[:, 0:16], side[:, head : head + 16], jnp.zeros((cols, 51), f32)], axis=1
+        [jnp.transpose(vec[...]), side[:, 0:16], side[:, head : head + 16], jnp.zeros((cols, 51), f32)], axis=1
     ))
     wm[...] = rounded(mod, 6 * width)
     for r in range(2):
@@ -844,6 +844,9 @@
     )(*args)
 
 
+ACROSS_FIRST = 2
+
+
 def gather_kernel(n, pa, pb, pf, pw, py, pm, pt, wa, wb, wf, ww, wy, wm, wt,
                   send, recv, crecv, own):
     pair = 2 if n % 2 == 0 else 1
@@ -906,11 +909,14 @@
         sem = crecv if way == 3 else recv
         return remote(src if is_own else there, there, send.at[way, i, o], sem.at[i, o], target)
 
-    def forward(o, up, down, side, wait):
+    def forward(o, up, down, side, wait, ways=None):
         is_own = not wait
         for item, when, common in parts:
 
-            def act(item=item, common=common):
+            def act(item=item, common=common, up=up, down=down, side=side):
+                if item[0] == ACROSS_FIRST and pair == 2:
+                    side = is_own
+                    up, down = (up, down) if ways is None else ways
                 if wait:
                     move(item, 0, o, across).wait_recv()
 
@@ -954,17 +960,18 @@
 
             if pair == 2:
 
-                def from_side(o, carry):
-                    forward(o * pair + other, None, None, False, True)
-                    return carry
+                def from_side(o, up, down):
+                    forward(o * pair + other, None, None, False, True, (up, down))
 
                 @pl.when(a - (k - 1) >= 0)
                 def _():
-                    from_side(a - (k - 1), 0)
+                    from_side(
+                        a - (k - 1), a < line - 1, jnp.logical_and(k == 1, a > 0)
+                    )
 
                 @pl.when(jnp.logical_and(k > 1, a + (k - 1) < line))
                 def _():
-                    from_side(a + (k - 1), 0)
+                    from_side(a + (k - 1), None, a > 0)
 
             return carry
 
@@ -975,14 +982,17 @@
     def drain(o, carry):
         there, column = o // pair, lax.rem(o, pair)
         mine = column == x
-        sent = (
-            (0, jnp.logical_and(mine, jnp.logical_and(there <= a, a < line - 1)), above),
-            (1, jnp.logical_and(mine, jnp.logical_and(there >= a, a > 0)), below),
-            (2, mine, across),
-        )
+        up = jnp.logical_and(there <= a, a < line - 1)
+        down = jnp.logical_and(there >= a, a > 0)
         for item, when, common in parts:
 
             def act(item=item, common=common):
+                lines_first = item[0] != ACROSS_FIRST or pair == 1
+                sent = (
+                    (0, jnp.logical_and(mine, up) if lines_first else up, above),
+                    (1, jnp.logical_and(mine, down) if lines_first else down, below),
+                    (2, mine if lines_first else o == d, across),
+                )
                 for way, yes, target in sent:
                     if way == 2 and pair == 1:
                         continue
@@ -1054,8 +1064,7 @@
 
     def row_copy(to, finish):
         value, there, qsend, qrecv = rows
-        slot = there.at[half] if from_role == 1 else there
-        copy = remote(value, slot, qsend.at[to], qrecv.at[half], dev(d, (1 - from_role) * 2 + to))
+        copy = remote(value, there, qsend.at[to], qrecv.at[half], dev(d, (1 - from_role) * 2 + to))
         copy.wait_send() if finish else copy.start()
 
     def row_sends(finish):
@@ -1064,12 +1073,8 @@
 
         @pl.when(role == from_role)
         def _():
-            if from_role == 0:
-                for to in range(2):
-                    pl.when(half == to)(functools.partial(row_copy, to, finish))
-            else:
-                for to in range(2):
-                    row_copy(to, finish)
+            for to in range(2):
+                pl.when(half == to)(functools.partial(row_copy, to, finish))
 
     row_sends(False)
     if swap is not None:
@@ -1110,11 +1115,7 @@
 
         @pl.when(role == 1 - from_role)
         def _():
-            if from_role == 0:
-                remote(value, there, qsend.at[0], qrecv.at[half], mate).wait_recv()
-            else:
-                for o in range(2):
-                    remote(value, there.at[o], qsend.at[0], qrecv.at[o], mate).wait_recv()
+            remote(value, there, qsend.at[0], qrecv.at[half], mate).wait_recv()
 
     if swap is not None:
 
@@ -1133,12 +1134,8 @@
             remote(own_src, own_dst, esend.at[0], erecv.at[0], dev(d, 2)).wait_recv()
 
 
-def backward_kernel(count, dh1, dkv, dmod, dhs, extra, dmods, send, recv, esend, erecv, qsend,
-                    qrecv):
-    relay_half_clips(
-        count, 1, dh1, dhs, send, recv, extra=(dkv.at[:, 0], extra, esend, erecv),
-        rows=(dmod, dmods, qsend, qrecv),
-    )
+def backward_kernel(count, dh1, dkv, dhs, extra, send, recv, esend, erecv):
+    relay_half_clips(count, 1, dh1, dhs, send, recv, extra=(dkv.at[:, 0], extra, esend, erecv))
 
 
 def swap_kernel(acts_s, acts_t, actf_s, actf_t, actw_s, actw_t, ybuf, dkvb, dy, dmod,
@@ -1151,8 +1148,10 @@
     gives = {
         (0, 0): [(0, actf_s, ractf), (1, actw_s, ractw), (4, dmod, rdmod)],
         (0, 1): [(0, acts_s, racts.at[pl.ds(0, six)]), (4, dmod, rdmod)],
-        (1, 0): [(0, actf_t, ractf), (1, actw_t, ractw), (2, dy, rdy)],
-        (1, 1): [(0, acts_t, racts), (1, ybuf, rybuf), (3, dkvb, rdkvb), (2, dy, rdy)],
+        (1, 0): [(0, actf_t, ractf), (1, actw_t, ractw), (2, dy, rdy), (4, dmod, rdmod)],
+        (1, 1): [
+            (0, acts_t, racts), (1, ybuf, rybuf), (3, dkvb, rdkvb), (2, dy, rdy), (4, dmod, rdmod)
+        ],
     }
     for (r, h), mine in gives.items():
 
@@ -1169,11 +1168,11 @@
 TEXT_CUTS = 11
 
 
-def scatter_kernel(n, own_in, snd, text_in, dm, vec, loss, wm, temb, ww, hid, wt,
+def scatter_kernel(n, own_in, snd, text_in, vec, dmod, rdmod, loss, wm, temb, ww, hid, wt,
                    summed, text, vsum, squares, gm, g2, g1,
-                   own, rx, up, down, sx, rz, tin, trx, tsx, trz, rv, rm, dtembs,
+                   own, rx, up, down, sx, rz, tin, trx, tsx, trz, rv, rm, dtembs, dm, dmt,
                    osem, send1, recv1, send2, recv2, usend, urecv, dsend, drecv,
-                   ssend, srecv, sown, tsend, trecv, esend, erecv):
+                   ssend, srecv, sown, tsend, trecv, esend, erecv, psend, precv):
     line = n // 2
     d, s = here()
     role, half = s // 2, lax.rem(s, 2)
@@ -1188,6 +1187,21 @@
     is_text, is_last, is_time = role == 0, s == 3, s == 0
     clip_rows = dm.shape[0]
 
+    def clip_sums():
+        clips = dmod.shape[0]
+        sources = (dmod, rdmod)
+        for clip in range(clips):
+            total = None
+            for h in range(2):
+                for i in range(clips):
+                    if (h * clips + i) // 2 == clip:
+                        part = sources[h][i]
+                        total = part if total is None else total + part
+            dm[8 * clip : 8 * clip + 8] = total
+
+    pl.when(half == 0)(clip_sums)
+    partial = remote(dm, dmt, psend.at[0], precv.at[0], other)
+
     def first_copies(u):
         return (
             remote(snd.at[u], rx.at[u], send1.at[u], recv1.at[u], across),
@@ -1226,9 +1240,14 @@
         copy = pltpu.make_async_copy(src(d), dst(d), sown.at[i])
         copy.wait() if finish else copy.start()
 
-    pl.when(is_time)(lambda: small(0, False))
     lax.fori_loop(0, 1, begin, 0)
     small(1, False)
+
+    @pl.when(is_time)
+    def _():
+        partial.wait_recv()
+        dm[...] = dm[...] + dmt[...]
+
     lax.fori_loop(1, count, begin, 0)
 
     @pl.when(is_last)
@@ -1237,6 +1256,7 @@
 
     @pl.when(role == 1)
     def _():
+        pl.when(half == 0)(lambda: partial.start())
         lax.fori_loop(0, TEXT_CUTS, lambda k, c: (text_hop(k).start(), c)[1], 0)
 
     def embeds(finish):
@@ -1326,6 +1346,8 @@
         def _():
             pairs(i)
 
+        pl.when(jnp.logical_and(is_time, i == 0))(lambda: small(0, False))
+
         @pl.when(jnp.logical_and(is_time, i == 1))
         def _():
             small(0, True)
@@ -1336,8 +1358,9 @@
         @pl.when(is_text)
         def _():
             def cut_at(delay, act):
-                k = i - delay
-                pl.when(jnp.logical_and(k >= 0, k < TEXT_CUTS))(lambda: act(k))
+                for j in range(2):
+                    k = 2 * (i - delay) + j
+                    pl.when(jnp.logical_and(k >= 0, k < TEXT_CUTS))(functools.partial(act, k))
 
             def arrive(k):
                 text_hop(k).wait_recv()
@@ -1347,9 +1370,9 @@
                 text_across(k).wait()
                 tsx[k] = low(tin[k, :, x].astype(f32) + trx[k].astype(f32))
 
-            cut_at(4, lambda k: direct(k, tsx.at[k], trz.at[k], False))
-            cut_at(1, arrive)
-            cut_at(3, add)
+            cut_at(5, lambda k: direct(k, tsx.at[k], trz.at[k], False))
+            cut_at(3, arrive)
+            cut_at(4, add)
 
         k = i - count
 
@@ -1376,7 +1399,7 @@
 
         return carry
 
-    lax.fori_loop(0, jnp.maximum(count + line, TEXT_CUTS + 4), round_trip, 0)
+    lax.fori_loop(0, jnp.maximum(count + line, TEXT_CUTS // 2 + 6), round_trip, 0)
     small(1, True)
     vsum[...] = lax.fori_loop(0, n, lambda o, total: total + rv[o], jnp.zeros(vsum.shape, f32))
 
@@ -1387,6 +1410,7 @@
 
     @pl.when(role == 1)
     def _():
+        pl.when(half == 0)(lambda: partial.wait_send())
         lax.fori_loop(0, TEXT_CUTS, lambda k, c: (text_hop(k).wait_send(), c)[1], 0)
 
     def collect(u, carry):
@@ -1870,8 +1894,8 @@
 def adamw_update(weight, first, second, grad, fix_one, fix_two):
     first = beta_one * first + (1.0 - beta_one) * grad
     second = beta_two * second + (1.0 - beta_two) * grad * grad
-    first_hat = first / fix_one
-    second_hat = second / fix_two
+    first_hat = first * fix_one
+    second_hat = second * fix_two
     weight = weight - adam_rate * (
         first_hat / (jnp.sqrt(second_hat) + 1e-08) + weight_decay * weight
     )
@@ -1881,11 +1905,17 @@
 def update_kernel(
     rates, pieces, scal, stat,
     aw, am, ag, ax, fw, fm, fg, fx, sw, s1, s2, gv, g1, g2, gt, gy2, gm, vw, v1, v2, gvall, gtall,
-    aw_, am_, ab_, fw_, fm_, fb_, sw_, s1_, s2_, sb_, vw_, v1_, v2_, vb_, loss_, norm_,
+    aw_, am_, ab_, fw_, fm_, fb_, sw_, s1_, s2_, sb_, vw_, v1_, v2_, vb_, loss_, norm_, powers,
 ):
     grad_norm = jnp.sqrt(stat[0:1, 0:1])
     factor = jnp.minimum(1.0, max_norm / (grad_norm + 1e-06))
-    fix_one, fix_two = scal[0], scal[1]
+
+    @pl.when(pl.program_id(0) == 0)
+    def _():
+        for i, beta in enumerate((beta_one, beta_two)):
+            powers[i] = lax.fori_loop(0, scal[0], lambda _, value: value * beta, jnp.float32(1.0))
+
+    fix_one, fix_two = (1.0 / (1.0 - jnp.full((1, 1), powers[i])) for i in range(2))
     loss_[...] = stat[4:5, 0:1]
     norm_[...] = grad_norm
     shrink = 1.0 - muon_rate * weight_decay
@@ -1985,7 +2015,7 @@
             sds((cols, six), bf16),
         ],
         [SM] * 2 + [VM] * 4,
-        (role_s, half_s, att_t, feed_t, side_t, vector_weights.T),
+        (role_s, half_s, att_t, feed_t, side_t, vector_weights),
     )
     freqs = jnp.exp(-math.log(10000.0) * jnp.arange(128, dtype=f32) / 128)
     angles = timesteps.astype(f32)[:, None] * freqs[None, :]
@@ -2134,16 +2164,12 @@
         ),
         [pltpu.VMEM((ncl, KP, width), bf16), pltpu.VMEM((ncl, KP, width), bf16)],
     )
-    dhs, extra, dmods_t = comm_call(
+    dhs, extra = comm_call(
         functools.partial(backward_kernel, count),
         4,
-        (dh1, dkv, dmod_t),
-        [
-            sds((count, 2, 64, width), bf16),
-            sds((2, LP, width), f32),
-            sds((2, count, 8, width), f32),
-        ],
-        [(count, 2), (count, 2), (1,), (1,), (2,), (2,)],
+        (dh1, dkv),
+        [sds((count, 2, 64, width), bf16), sds((2, LP, width), f32)],
+        [(count, 2), (count, 2), (1,), (1,)],
     )
     acts_s, actf_s, actw_s, dkvb, dy, vect, dmod = local_call(
         last_kernel,
@@ -2209,26 +2235,13 @@
         ],
     )
 
-    mine0 = jnp.where(half == 0, dmod, rdmod)
-    mine1 = jnp.where(half == 0, rdmod, dmod)
-    sources = (mine0, mine1, dmods_t[0], dmods_t[1])
-    dm_clip = []
-    for clip in range(count):
-        total = 0.0
-        for seg in range(4):
-            for i in range(count):
-                if ((seg % 2) * count + i) // 2 == clip:
-                    total = total + sources[seg][i]
-        dm_clip.append(total)
-    dm = jnp.concatenate(dm_clip, axis=0)
-
     whole_clips = n * 8
     text_block = (TEXT_CUTS, line, own_rows, cut_text)
     summed, text_sum, vsum, tile, grad_mod, grad_time2, grad_time1 = comm_call(
         functools.partial(scatter_kernel, n),
         6,
         (
-            grad_own, grad_snd, text_part, dm, vect.reshape(n, cols, 128), loss_t,
+            grad_own, grad_snd, text_part, vect.reshape(n, cols, 128), dmod, rdmod, loss_t,
             wm_own, temb, ww, hid, wt.reshape(whole_clips, width),
         ),
         [
@@ -2243,9 +2256,9 @@
         [(9,), (9 + TEXT_CUTS,), (9 + TEXT_CUTS,)]
         + [(TEXT_CUTS + 1, line)] * 2
         + [(8, line)] * 4
-        + [(2, n), (2, n), (2,), (TEXT_CUTS,), (TEXT_CUTS,), (n,), (n,)],
+        + [(2, n), (2, n), (2,), (TEXT_CUTS,), (TEXT_CUTS,), (n,), (n,), (1,), (1,)],
         [VM] * 7,
-        in_specs=[ANY] * 5 + [VM] * 6,
+        in_specs=[ANY] * 4 + [VM] * 8,
         scratch=[
             pltpu.VMEM(block, f32),
             pltpu.VMEM(block, bf16),
@@ -2260,6 +2273,8 @@
             pltpu.VMEM((n, cols, 128), f32),
             pltpu.VMEM((n * 8 * count, width), f32),
             pltpu.VMEM((n, whole_clips, 128), f32),
+            pltpu.VMEM((8 * count, width), f32),
+            pltpu.VMEM((8 * count, width), f32),
         ],
     )
 
@@ -2315,8 +2330,6 @@
         [(n,), (8,), (23, 3), (23, 3), (8,), (3,)],
     )
 
-    clock = step_count[0].astype(f32)
-    scal = jnp.stack([1.0 - jnp.power(beta_one, clock), 1.0 - jnp.power(beta_two, clock)])
     text_grad = gy12.reshape(2 * own_rows, wide_text)[:cols]
     side_m, side_v = side_first.T, side_second.T
     side_rows = side_t.shape[1]
@@ -2368,8 +2381,9 @@
         out_shape=row_outs + whole_outs,
         in_specs=[SM, whole_spec(stat)] + [rows_spec(v) for v in cutup] + [whole_spec(v) for v in fixed],
         out_specs=[rows_spec(v) for v in row_outs] + [whole_spec(v) for v in whole_outs],
+        scratch_shapes=[pltpu.SMEM((2,), f32)],
         compiler_params=pltpu.CompilerParams(vmem_limit_bytes=VMEM_LIMIT),
-    )(scal, stat, *cutup, *fixed)
+    )(step_count, stat, *cutup, *fixed)
 
     def att(value):
         return value.reshape(att_t.shape)

time: 323 us -> 316 us (0.978)
  Pallas kernels: 305 us -> 301 us
    pallas_call x8, Pallas kernels: 220 us -> 216 us  [comm_call(): pl.pallas_call(kernel, out_shape=out_shape, in_specs=[ANY] * len(args) if...]
where the time goes in v1:
time: 316 us; the launch traced here: 313 us
  Pallas kernels  301 us (95%)
  local copies, waits for them, and re-layouts  8.62 us (3%)
    pallas_call x8, Pallas kernels, comm_call(): pl.pallas_call(kernel, out_shape=out_shape, in_specs=[ANY] * len(args) if...  216 us
    pallas_call x7, Pallas kernels, local_call(): pl.pallas_call(kernel, out_shape=out_shape, in_specs=in_specs, out_specs=...  73.4 us
    pallas_call x1, Pallas kernels, body(): pl.pallas_call(functools.partial(update_kernel, rates, pieces), grid=(gri...  11.4 us

profile of v1, /device:TPU:27, one launch (start us, length us, event | category | flops | bytes accessed | tf_op | source)
XLA Modules:
  0.0 313.5 jit_solution(1668549629379246600)
XLA Ops:
  0.7 0.0 copy-start.2
  0.7 3.4 %shard_map.298 = (bf16[4,48,384]{2,1,0:T(8,128)(2,1)}, bf16[4,48,384]{2,1,0:T(8,128)(2,1)}, bf16[2,192,384]{2,1,0:T(8,128)(2,1)}, bf16[48,1152]{1,0:T(8,128)(2,1...) custom-call(s32[1]{0:T(128)} %bitcast.7.role, s32[1]{0:T(128)} %bitcast.8.half, ...), custom_call_target="tpu_custom_call" | custom-call | tf_op jit(solution)/shard_map/pallas_call | solution.py:784
  4.1 0.0 copy-done.2
  4.1 0.1 multiply_cosine_fusion
  4.2 0.1 fusion.2
  4.3 0.1 copy.50
  4.4 0.6 select_maximum_fusion.pt
  5.0 37.2 %shard_map.299 = (bf16[4,8,48,384]{3,2,1,0:T(8,128)(2,1)}, bf16[4,8,48,384]{3,2,1,0:T(8,128)(2,1)}, bf16[2,8,192,384]{3,2,1,0:T(8,128)(2,1)}, bf16[8,48,1152]{2,...) custom-call(bf16[4,48,384]{2,1,0:T(8,128)(2,1)} %get-tuple-element.140.pa, ...), custom_call_target="tpu_custom_call" | custom-call | tf_op jit(solution)/shard_map/pallas_call | solution.py:835
  42.2 3.1 shard_map.300
  45.3 3.0 shard_map.301.mq
  48.3 0.0 copy-done
  48.3 8.9 %conditional.2 = (bf16[384,128]{1,0:T(8,128)(2,1)}) conditional(s32[]{:T(128)} %convert_element_type.19, () %tuple.22, (f32[3]{0:T(128)S(1)}, f32[3,4,4,16,16]{4,3,2,1,0:T(8,128)S(1)}, f32[3,4,4,16,16]{4,3,2,1,0:T(8,128)S(1)}, s32[]{:T(128)}) %tuple.44), branch_computations={%region_0.1_spmd, %region_1.2_spmd} | conditional | flops 49159 | bytes 577656 | solution.py:2082
  48.4 1.2 copy.48
  49.6 1.2 copy.49
  50.8 1.2 add_convert_fusion
  51.9 3.9 %copy.45 = bf16[3,4,8,8,2,2,4]{3,2,1,0,6,5,4:T(8,128)(2,1)S(1)} copy(bf16[3,4,8,8,2,2,4]{6,5,3,4,2,1,0:T(2,128)(2,1)} %bitcast.101) | data formatting | bytes 49152 | tf_op jit(solution)/shard_map/cond/branch_1_fun/transpose | solution.py:63
  55.9 0.5 reshape.117
  56.4 0.1 copy.57
  56.5 0.8 pad.9.clone
  57.3 11.9 %shard_map.302 = (bf16[3,2,64,384]{3,2,1,0:T(8,128)(2,1)}, f32[3,304,192]{2,1,0:T(8,128)}, bf16[3,304,192]{2,1,0:T(8,128)(2,1)}, bf16[5,384,384]{2,1,0:T(8,128)(...) custom-call(s32[1]{0:T(128)} %bitcast.7.role, s32[1]{0:T(128)} %bitcast.8.half, ...), custom_call_target="tpu_custom_call" | custom-call | tf_op jit(solution)/shard_map/pallas_call | solution.py:784
  69.2 13.6 %shard_map.303 = (bf16[3,2,64,384]{3,2,1,0:T(8,128)(2,1)}, bf16[3,304,192]{2,1,0:T(8,128)(2,1)}, f32[2,8,1152]{2,1,0:T(8,128)}) custom-call(bf16[3,2,64,384]{3,2,1,0:T(8,128)(2,1)} %get-tuple-element.163.h1s, bf16[3,304,192]{2,1,0:T(8,128)(2,1)} %get-tuple-element.164.gq, f32[2,8,1152]{2,1,0:T(8,128)} %shard_map.301.mq), custom_call_target="tpu_custom_call" | custom-call | tf_op jit(solution)/shard_map/pallas_call | solution.py:835
  82.8 0.8 copy.53.target
  83.6 6.6 %shard_map.304 = (bf16[3,2,64,384]{3,2,1,0:T(8,128)(2,1)}, bf16[10,384,384]{2,1,0:T(8,128)(2,1)}, bf16[2,384,384]{2,1,0:T(8,128)(2,1)}, bf16[2,384,1536]{2,1,0:T...) custom-call(s32[1]{0:T(128)} %bitcast.7.role, ...), custom_call_target="tpu_custom_call" | custom-call | tf_op jit(solution)/shard_map/pallas_call | solution.py:784
  90.2 36.5 %shard_map.305 = (bf16[3,2,64,384]{3,2,1,0:T(8,128)(2,1)}, f32[2,304,384]{2,1,0:T(8,128)}) custom-call(bf16[3,2,64,384]{3,2,1,0:T(8,128)(2,1)} %get-tuple-element.171.dh1, f32[2,2,304,384]{3,2,1,0:T(8,128)} %get-tuple-element.172.dkv), custom_call_target="tpu_custom_call" | custom-call | tf_op jit(solution)/shard_map/pallas_call | solution.py:835
  126.7 16.4 %shard_map.306 = (bf16[6,384,384]{2,1,0:T(8,128)(2,1)}, bf16[2,384,384]{2,1,0:T(8,128)(2,1)}, bf16[2,384,1536]{2,1,0:T(8,128)(2,1)}, bf16[2,2,304,384]{3,2,1,0:T...) custom-call(s32[1]{0:T(128)} %bitcast.7.role, s32[1]{0:T(128)} %bitcast.8.half, ...), custom_call_target="tpu_custom_call" | custom-call | tf_op jit(solution)/shard_map/pallas_call | solution.py:784
  143.1 5.9 %shard_map.307 = (bf16[10,384,384]{2,1,0:T(8,128)(2,1)}, bf16[2,384,384]{2,1,0:T(8,128)(2,1)}, bf16[2,384,1536]{2,1,0:T(8,128)(2,1)}, bf16[2,304,384]{2,1,0:T(8,...) custom-call(bf16[6,384,384]{2,1,0:T(8,128)(2,1)} %get-tuple-element.177.acts_s, ...), custom_call_target="tpu_custom_call" | custom-call | tf_op jit(solution)/shard_map/pallas_call | solution.py:835
  149.0 12.3 %shard_map.308 = (f32[9,4,48,384]{3,2,1,0:T(8,128)}, bf16[9,4,48,384]{3,2,1,0:T(8,128)(2,1)}, bf16[4,2,24,4224]{3,2,1,0:T(8,128)(2,1)}) custom-call(s32[1]{0:T(128)} %bitcast.7.role, s32[1]{0:T(128)} %bitcast.8.half, s32[1]{0:T(128)} %bitcast.9.rank, bf16[6,384,384]{2,1,0:T(8,128)(2,1)} %get-tuple-element.177.acts_s, ...), custom_call_target="tpu_custom_call" | custom-call | tf_op jit(solution)/shard_map/pallas_call | solution.py:784
  161.3 70.7 %shard_map.309 = (f32[9,48,384]{2,1,0:T(8,128)}, bf16[24,4224]{1,0:T(8,128)(2,1)}, f32[48,128]{1,0:T(8,128)}, f32[8,384]{1,0:T(8,128)}, f32[48,2304]{1,0:T(8,128...) custom-call(f32[9,4,48,384]{3,2,1,0:T(8,128)} %get-tuple-element.194.own_in, bf16[9,4,48,384]{3,2,1,0:T(8,128)(2,1)} %get-tuple-element.195.snd, ...), custom_call_target="tpu_custom_call" | custom-call | tf_op jit(solution)/shard_map/pallas_call | solution.py:835
  232.0 21.9 %shard_map.310 = (f32[8,48,384]{2,1,0:T(8,128)}, f32[8,4,48,384]{3,2,1,0:T(8,128)}, f32[12,48,384]{2,1,0:T(8,128)}, f32[16,48,384]{2,1,0:T(8,128)}, f32[48,2304]...) custom-call(f32[48,128]{1,0:T(8,128)} %get-tuple-element.202.vsum, ...), custom_call_target="tpu_custom_call" | custom-call | tf_op jit(solution)/shard_map/pallas_call | solution.py:835
  254.0 19.8 %shard_map.311 = (bf16[384,384]{1,0:T(8,128)(2,1)}, bf16[1536,384]{1,0:T(8,128)(2,1)}) custom-call(s32[1]{0:T(128)} %bitcast.8.half, f32[384,384]{1,0:T(8,128)} %bitcast.113, f32[1536,384]{1,0:T(8,128)} %bitcast.102), custom_call_target="tpu_custom_call" | custom-call | tf_op jit(solution)/shard_map/pallas_call | solution.py:784
  273.8 27.5 %shard_map.312 = (bf16[12,48,384]{2,1,0:T(8,128)(2,1)}, bf16[4,192,384]{2,1,0:T(8,128)(2,1)}, bf16[2,24,4224]{2,1,0:T(8,128)(2,1)}, f32[48,384]{1,0:T(8,128)}) custom-call(bf16[8,48,384]{2,1,0:T(8,128)(2,1)} %bitcast.118, bf16[8,192,384]{2,1,0:T(8,128)(2,1)} %bitcast.108, bf16[24,4224]{1,0:T(8,128)(2,1)} %get-tuple-element.214.gy1, ...), custom_call_target="tpu_custom_call" | custom-call | tf_op jit(solution)/shard_map/pallas_call | solution.py:835
  301.9 11.4 %shard_map.313 = (f32[576,384]{1,0:T(8,128)}, f32[576,384]{1,0:T(8,128)}, bf16[576,384]{1,0:T(8,128)(2,1)}, f32[768,384]{1,0:T(8,128)}, f32[768,384]{1,0:T(8,128...) custom-call(s32[1]{0:T(128)S(6)} %copy.62.scal, ...), custom_call_target="tpu_custom_call" | custom-call | tf_op jit(solution)/shard_map/pallas_call | solution.py:2378
  (9 shorter events, 0.1 us)
Async XLA Ops:
  0.7 3.4 %copy-start.2 = (s32[3]{0:T(128)S(1)}, s32[3]{0:T(128)}, u32[]{:S(2)}) copy-start(s32[3]{0:T(128)} %param.24) | copy-start | bytes 40
  4.1 44.2 %copy-start = (f32[3,4,4,16,16]{4,3,2,1,0:T(8,128)S(1)}, f32[3,4,4,16,16]{4,3,2,1,0:T(8,128)}, u32[]{:S(2)}) copy-start(f32[3,4,4,16,16]{4,3,2,1,0:T(8,128)} %param.23) | copy-start | bytes 147460
  4.1 44.2 %copy-start.1 = (f32[3,4,4,16,16]{4,3,2,1,0:T(8,128)S(1)}, f32[3,4,4,16,16]{4,3,2,1,0:T(8,128)}, u32[]{:S(2)}) copy-start(f32[3,4,4,16,16]{4,3,2,1,0:T(8,128)} %param.22) | copy-start | bytes 147460

commit v2 on v1

--- a/solution.py
+++ b/solution.py
@@ -55,13 +55,6 @@
     level = jnp.cos((steps_t / 1000.0 + 0.008) / 1.008 * (math.pi / 2)) ** 2
     ratio = level / (1.0 - level)
     return level, jnp.minimum(ratio, snr_gamma) / ratio
-
-
-def patchify(frames):
-    clips, count, channels, height, breadth = frames.shape
-    grid = frames.reshape(clips, count, channels, height // 2, 2, breadth // 2, 2)
-    grid = grid.transpose(0, 1, 3, 5, 4, 6, 2)
-    return grid.reshape(clips, count, (height // 2) * (breadth // 2), 4 * channels)
 
 
 def sincos(places, model_width):
@@ -279,10 +272,35 @@
     errs[...] = jnp.broadcast_to(weight, errs.shape)
 
 
-def embed_chunk(tok_ref, vec, pos_ref, chunk):
-    tokens = tok_ref[pl.ds(pl.multiple_of(chunk * 128, 128), 128), :]
+class Patches:
+    def __init__(self, rows, first, lane0):
+        place = lax.broadcasted_iota(jnp.int32, (rows, 16), 0)
+        col = lax.broadcasted_iota(jnp.int32, (rows, 16), 1)
+        self.pick = [low(jnp.where(col == 2 * (place % 8) + q, 1.0, 0.0)) for q in range(2)]
+        place = lax.broadcasted_iota(jnp.int32, (rows, 64), 0)
+        line = lax.broadcasted_iota(jnp.int32, (rows, 64), 1) % 16
+        self.keep = [line == 2 * (first + place // 8) + p for p in range(2)]
+        channel = lax.broadcasted_iota(jnp.int32, (64, 128), 0) // 16
+        lane = lax.broadcasted_iota(jnp.int32, (64, 128), 1) - lane0
+        self.put = [
+            [low(jnp.where(lane == p * 8 + q * 4 + channel, 1.0, 0.0)) for q in range(2)]
+            for p in range(2)
+        ]
+
+    def of(self, pieces):
+        total = None
+        for piece in pieces:
+            for q in range(2):
+                columns = nt(self.pick[q], piece)
+                for p in range(2):
+                    part = nn(low(jnp.where(self.keep[p], columns, 0.0)), self.put[p][q])
+                    total = part if total is None else total + part
+        return total
+
+
+def embed_chunk(tokens, vec, pos_ref):
     places = pos_ref[...] + vec[0:1]
-    return low(nn(tokens, low(vec[...])) + jnp.concatenate([places, places], axis=0)), tokens
+    return low(nn(tokens, low(vec[...])) + jnp.concatenate([places, places], axis=0))
 
 
 def spatial_bias(vec):
@@ -303,8 +321,8 @@
 
 
 def first_kernel(
-    cols, role, half, tok, pos, mq, vec, wa, wf, wy, captions,
-    h1, hq, gq, out_b, out_f, out_u, out_p, kept_b, kept_f, kept_u, kept_p, cap, sems, ksem,
+    cols, role, half, clean, noise, pt, pos, mq, vec, wa, wf, wy, captions,
+    h1, hq, gq, tok, out_b, out_f, out_u, out_p, kept_b, kept_f, kept_u, kept_p, cap, sems, ksem,
 ):
     @pl.when(role[0] == 1)
     def _():
@@ -328,6 +346,7 @@
         allowed = pair_mask(0)
         count = h1.shape[0]
         bu = up_bias(vec, 14)
+        patches = Patches(64, 0, EMB0)
         residuals = residual_copies((kept_b, kept_f, kept_u, kept_p), (out_b, out_f, out_u, out_p), ksem)
 
         def step(chunk, carry):
@@ -336,8 +355,18 @@
                 for copy in residuals(chunk - 1):
                     copy.start()
 
-            m = mod_rows(mq, vec, 19, (half[0] * count + chunk) // 2)
-            h0, _ = embed_chunk(tok, vec, pos, chunk)
+            there = half[0] * count + chunk
+            clip = there // 2
+            m = mod_rows(mq, vec, 19, clip)
+            mix = pt[pl.ds(clip, 1), :][:, 256:384]
+            frames = []
+            for f in range(2):
+                frame = 2 * lax.rem(there, 2) + f
+                one, two = (ref[clip, frame].reshape(64, 16) for ref in (clean, noise))
+                frames.append(patches.of([low(mix[:, 1:2] * one + mix[:, 2:3] * two)]))
+            tokens = low(jnp.concatenate(frames, axis=0))
+            tok[pl.ds(pl.multiple_of(chunk * 128, 128), 128), :] = tokens
+            h0 = embed_chunk(tokens, vec, pos)
             x1, kept = self_forward(h0.astype(f32), m, wa, spatial_bias(vec), allowed)
             x, kept_feed = feed_forward(x1, m, wf, bu, vec[18:19])
             out = low(x)
@@ -447,7 +476,7 @@
 
 
 def temporal_kernel(
-    role, half, rank, lens, errw, h1, timing, mq, vec, temb, wa, wb, wf, gq, rgq, y2p, target,
+    role, half, rank, lens, errw, h1, timing, mq, vec, temb, wa, wb, wf, gq, rgq, y2p, noise,
     dh1, acts, actf, actw, ybuf, dkv, grads, dmod, loss, kx, vx,
 ):
     @pl.when(role[0] == 0)
@@ -501,7 +530,15 @@
             normed, inv = norm(h2)
             cf = low(normed * (1.0 + m7) + m6)
             where = pl.ds(pl.multiple_of(chunk * 128, 128), 128)
-            diff = jnp.where(real, nt(cf, head) + bias_h - target[where, :], 0.0)
+            patches = Patches(32, 4 * lax.rem(half[0] * count + chunk, 2), HEAD0)
+            target = jnp.concatenate(
+                [
+                    patches.of(three(noise[clip, frame].reshape(64, 16)))
+                    for frame in range(noise.shape[1])
+                ],
+                axis=0,
+            )
+            diff = jnp.where(real, nt(cf, head) + bias_h - target, 0.0)
             scale = errw[pl.ds(clip, 1), 0:1]
             loss[...] += col_sum(diff * diff) * scale
             dpred = low(diff * (2.0 * scale))
@@ -763,15 +800,11 @@
             left = lefts(poly_of(a))
             both = nn(left, rights(jnp.concatenate([a, whole[...]], axis=1)))
             whole[...] = both[:, width:]
-
-            @pl.when(i < 4)
-            def _():
-                gram[...] = nn(left, rights(both[:, :width]))
-
+            gram[...] = nn(left, rights(both[:, :width]))
             return carry
 
-        lax.fori_loop(0, 5, sweep, 0)
-        last = rights(whole[...])
+        lax.fori_loop(0, 4, sweep, 0)
+        last = rights(nn(lefts(poly_of(gram[...])), rights(whole[...])))
 
         def apply(t, carry):
             xf[rows(t), :] = low(nn(lefts(uf[rows(t), :]), last))
@@ -844,7 +877,7 @@
     )(*args)
 
 
-ACROSS_FIRST = 2
+ACROSS_FIRST = (2, 5)
 
 
 def gather_kernel(n, pa, pb, pf, pw, py, pm, pt, wa, wb, wf, ww, wy, wm, wt,
@@ -914,7 +947,7 @@
         for item, when, common in parts:
 
             def act(item=item, common=common, up=up, down=down, side=side):
-                if item[0] == ACROSS_FIRST and pair == 2:
+                if item[0] in ACROSS_FIRST and pair == 2:
                     side = is_own
                     up, down = (up, down) if ways is None else ways
                 if wait:
@@ -987,7 +1020,7 @@
         for item, when, common in parts:
 
             def act(item=item, common=common):
-                lines_first = item[0] != ACROSS_FIRST or pair == 1
+                lines_first = item[0] not in ACROSS_FIRST or pair == 1
                 sent = (
                     (0, jnp.logical_and(mine, up) if lines_first else up, above),
                     (1, jnp.logical_and(mine, down) if lines_first else down, below),
@@ -2020,8 +2053,9 @@
     freqs = jnp.exp(-math.log(10000.0) * jnp.arange(128, dtype=f32) / 128)
     angles = timesteps.astype(f32)[:, None] * freqs[None, :]
     level, snr = snr_weight(timesteps.astype(f32))
-    pt = jnp.concatenate([jnp.cos(angles), jnp.sin(angles), snr[:, None]], axis=1)
-    pt = jnp.pad(pt, ((0, 8 - count), (0, width - 257)))
+    mix = jnp.stack([snr, jnp.sqrt(level), jnp.sqrt(1.0 - level)], axis=1)
+    pt = jnp.concatenate([jnp.cos(angles), jnp.sin(angles), mix], axis=1)
+    pt = jnp.pad(pt, ((0, 8 - count), (0, width - 259)))
 
     wa, wb, wf, ww, wy, wm, wt = comm_call(
         functools.partial(gather_kernel, n),
@@ -2064,28 +2098,6 @@
     )
 
     half_tokens = count * per_clip // 2
-
-    def own_rows_of(value):
-        return lax.dynamic_slice_in_dim(
-            value.reshape(count * per_clip, 16), half * half_tokens, half_tokens, 0
-        )
-
-    def tokens(clean, noise):
-        mix = level[:, None, None, None, None]
-        noisy = low(jnp.sqrt(mix) * clean + jnp.sqrt(1.0 - mix) * noise)
-        return jnp.pad(own_rows_of(patchify(noisy)), ((0, 0), (EMB0, 112 - EMB0)))
-
-    def targets(noise):
-        value = patchify(noise).reshape(count, frames, 2, 32, 16).transpose(0, 2, 1, 3, 4)
-        return jnp.pad(own_rows_of(value), ((0, 0), (HEAD0, 112 - HEAD0)))
-
-    tok = lax.cond(
-        role == 0,
-        tokens,
-        lambda clean, noise: jnp.zeros((half_tokens, 128), bf16),
-        latents,
-        noise_draw,
-    )
     places = np.arange(per_clip // frames)
     edge = latents.shape[3] // 2
     pos = np.concatenate(
@@ -2102,32 +2114,25 @@
         sds((count, 3, 256, 128), f32),
     ]
     residual_scratch = [pltpu.VMEM(v.shape, v.dtype) for v in residuals]
-    h1s, hq, gq_own, kept_b, kept_f, kept_u, kept_p = local_call(
+    h1s, hq, gq_own, tok, kept_b, kept_f, kept_u, kept_p = local_call(
         functools.partial(first_kernel, cols),
         [
             sds((count, 2, 64, width), bf16),
             sds((count, LP, lanes), f32),
             sds((count, LP, lanes), bf16),
+            sds((half_tokens, 128), bf16),
         ]
         + residuals,
-        [SM] * 2 + [VM] * 7 + [ANY],
-        (role_s, half_s, tok, pos, mq, vec, wa, wf, wy, captions),
+        [SM] * 2 + [VM] * 9 + [ANY],
+        (role_s, half_s, latents, noise_draw, pt, pos, mq, vec, wa, wf, wy, captions),
         residual_scratch
         + [
             pltpu.VMEM((count, clip_rows, text), bf16),
             pltpu.SemaphoreType.DMA((count,)),
             pltpu.SemaphoreType.DMA((count, 4)),
         ],
-        [VM] * 3 + [ANY] * 4,
+        [VM] * 4 + [ANY] * 4,
     )
-    later_noise, gq_own = lax.optimization_barrier((noise_draw, gq_own))
-    target = lax.cond(
-        role == 1,
-        targets,
-        lambda noise: jnp.zeros((half_tokens, 128), f32),
-        later_noise,
-    )
-    target, h1s = lax.optimization_barrier((target, h1s))
     h1t, rgq, mqt = comm_call(
         functools.partial(forward_kernel, count),
         3,
@@ -2160,7 +2165,7 @@
         [SM] * 4 + [VM] * 13,
         (
             role_s, half_s, rank_s, caption_len, errs, h1t, timing, mqt, vec, temb, wa, wb, wf,
-            gq_own, rgq, y2p, target,
+            gq_own, rgq, y2p, noise_draw,
         ),
         [pltpu.VMEM((ncl, KP, width), bf16), pltpu.VMEM((ncl, KP, width), bf16)],
     )

time: 316 us -> 309 us (0.978)
  local copies, waits for them, and re-layouts: 8.62 us -> 0.99 us
    transpose x1 -> x0, local copies, waits for them, and re-layouts: 3.91 us -> none  [patchify(): grid = grid.transpose(0, 1, 3, 5, 4, 6, 2)]
where the time goes in v2:
time: 309 us; the launch traced here: 307 us
  Pallas kernels  304 us (98%)
    pallas_call x8, Pallas kernels, comm_call(): pl.pallas_call(kernel, out_shape=out_shape, in_specs=[ANY] * len(args) if...  219 us
    pallas_call x7, Pallas kernels, local_call(): pl.pallas_call(kernel, out_shape=out_shape, in_specs=in_specs, out_specs=...  73.4 us
    pallas_call x1, Pallas kernels, body(): pl.pallas_call(functools.partial(update_kernel, rates, pieces), grid=(gri...  11.4 us

profile of v2, /device:TPU:27, one launch (start us, length us, event | category | flops | bytes accessed | tf_op | source)
XLA Modules:
  0.0 306.5 jit_solution(6180083779995310964)
XLA Ops:
  0.7 0.0 copy-start
  0.7 3.4 %shard_map.297 = (bf16[4,48,384]{2,1,0:T(8,128)(2,1)}, bf16[4,48,384]{2,1,0:T(8,128)(2,1)}, bf16[2,192,384]{2,1,0:T(8,128)(2,1)}, bf16[48,1152]{1,0:T(8,128)(2,1...) custom-call(s32[1]{0:T(128)} %bitcast.role, s32[1]{0:T(128)} %bitcast.1.half, ...), custom_call_target="tpu_custom_call" | custom-call | tf_op jit(solution)/shard_map/pallas_call | solution.py:817
  4.1 0.0 copy-done
  4.2 0.1 copy.34
  4.3 0.1 copy.35
  4.4 0.1 multiply_sine_fusion
  4.5 0.1 copy.36
  4.6 0.1 concatenate.3
  4.7 0.6 pad.4.pt
  5.3 37.2 %shard_map.298 = (bf16[4,8,48,384]{3,2,1,0:T(8,128)(2,1)}, bf16[4,8,48,384]{3,2,1,0:T(8,128)(2,1)}, bf16[2,8,192,384]{3,2,1,0:T(8,128)(2,1)}, bf16[8,48,1152]{2,...) custom-call(bf16[4,48,384]{2,1,0:T(8,128)(2,1)} %get-tuple-element.113.pa, ...), custom_call_target="tpu_custom_call" | custom-call | tf_op jit(solution)/shard_map/pallas_call | solution.py:868
  42.5 3.1 %shard_map.299 = (f32[128,384]{1,0:T(8,128)}, f32[64,384]{1,0:T(8,128)}, f32[64,384]{1,0:T(8,128)}, f32[8,1152]{1,0:T(8,128)}, bf16[2,384,192]{2,1,0:T(8,128)(2,1)}, /*index=5*/f32[8,128]{1,0:T(8,128)}) custom-call(s32[1]{0:T(128)} %bitcast.2.rank, f32[64,384]{1,0:T(8,128)} %bitcast.100, bf16[384,1152]{1,0:T(8,128)(2,1)} %bitcast.81, bf16[384,1152]{1,0:T(8,128)(2,1)} %bitcast.95), custom_call_target="tpu_custom_call" | custom-call | tf_op jit(solution)/shard_map/pallas_call | solution.py:817
  45.6 3.0 shard_map.300.mq
  48.6 13.2 %shard_map.301 = (bf16[3,2,64,384]{3,2,1,0:T(8,128)(2,1)}, f32[3,304,192]{2,1,0:T(8,128)}, bf16[3,304,192]{2,1,0:T(8,128)(2,1)}, bf16[384,128]{1,0:T(8,128)(2,1)...) custom-call(s32[1]{0:T(128)} %bitcast.role, ...), custom_call_target="tpu_custom_call" | custom-call | tf_op jit(solution)/shard_map/pallas_call | solution.py:817
  61.8 15.2 %shard_map.302 = (bf16[3,2,64,384]{3,2,1,0:T(8,128)(2,1)}, bf16[3,304,192]{2,1,0:T(8,128)(2,1)}, f32[2,8,1152]{2,1,0:T(8,128)}) custom-call(bf16[3,2,64,384]{3,2,1,0:T(8,128)(2,1)} %get-tuple-element.134.h1s, bf16[3,304,192]{2,1,0:T(8,128)(2,1)} %get-tuple-element.135.gq, f32[2,8,1152]{2,1,0:T(8,128)} %shard_map.300.mq), custom_call_target="tpu_custom_call" | custom-call | tf_op jit(solution)/shard_map/pallas_call | solution.py:868
  77.1 6.7 %shard_map.303 = (bf16[3,2,64,384]{3,2,1,0:T(8,128)(2,1)}, bf16[10,384,384]{2,1,0:T(8,128)(2,1)}, bf16[2,384,384]{2,1,0:T(8,128)(2,1)}, bf16[2,384,1536]{2,1,0:T...) custom-call(s32[1]{0:T(128)} %bitcast.role, ...), custom_call_target="tpu_custom_call" | custom-call | tf_op jit(solution)/shard_map/pallas_call | solution.py:817
  83.7 37.6 %shard_map.304 = (bf16[3,2,64,384]{3,2,1,0:T(8,128)(2,1)}, f32[2,304,384]{2,1,0:T(8,128)}) custom-call(bf16[3,2,64,384]{3,2,1,0:T(8,128)(2,1)} %get-tuple-element.141.dh1, f32[2,2,304,384]{3,2,1,0:T(8,128)} %get-tuple-element.142.dkv), custom_call_target="tpu_custom_call" | custom-call | tf_op jit(solution)/shard_map/pallas_call | solution.py:868
  121.3 16.4 %shard_map.305 = (bf16[6,384,384]{2,1,0:T(8,128)(2,1)}, bf16[2,384,384]{2,1,0:T(8,128)(2,1)}, bf16[2,384,1536]{2,1,0:T(8,128)(2,1)}, bf16[2,2,304,384]{3,2,1,0:T...) custom-call(s32[1]{0:T(128)} %bitcast.role, s32[1]{0:T(128)} %bitcast.1.half, ...), custom_call_target="tpu_custom_call" | custom-call | tf_op jit(solution)/shard_map/pallas_call | solution.py:817
  137.7 5.9 %shard_map.306 = (bf16[10,384,384]{2,1,0:T(8,128)(2,1)}, bf16[2,384,384]{2,1,0:T(8,128)(2,1)}, bf16[2,384,1536]{2,1,0:T(8,128)(2,1)}, bf16[2,304,384]{2,1,0:T(8,...) custom-call(bf16[6,384,384]{2,1,0:T(8,128)(2,1)} %get-tuple-element.147.acts_s, ...), custom_call_target="tpu_custom_call" | custom-call | tf_op jit(solution)/shard_map/pallas_call | solution.py:868
  143.6 12.3 %shard_map.307 = (f32[9,4,48,384]{3,2,1,0:T(8,128)}, bf16[9,4,48,384]{3,2,1,0:T(8,128)(2,1)}, bf16[4,2,24,4224]{3,2,1,0:T(8,128)(2,1)}) custom-call(s32[1]{0:T(128)} %bitcast.role, s32[1]{0:T(128)} %bitcast.1.half, s32[1]{0:T(128)} %bitcast.2.rank, bf16[6,384,384]{2,1,0:T(8,128)(2,1)} %get-tuple-element.147.acts_s, ...), custom_call_target="tpu_custom_call" | custom-call | tf_op jit(solution)/shard_map/pallas_call | solution.py:817
  155.9 71.0 %shard_map.308 = (f32[9,48,384]{2,1,0:T(8,128)}, bf16[24,4224]{1,0:T(8,128)(2,1)}, f32[48,128]{1,0:T(8,128)}, f32[8,384]{1,0:T(8,128)}, f32[48,2304]{1,0:T(8,128...) custom-call(f32[9,4,48,384]{3,2,1,0:T(8,128)} %get-tuple-element.164.own_in, bf16[9,4,48,384]{3,2,1,0:T(8,128)(2,1)} %get-tuple-element.165.snd, ...), custom_call_target="tpu_custom_call" | custom-call | tf_op jit(solution)/shard_map/pallas_call | solution.py:868
  226.9 21.9 %shard_map.309 = (f32[8,48,384]{2,1,0:T(8,128)}, f32[8,4,48,384]{3,2,1,0:T(8,128)}, f32[12,48,384]{2,1,0:T(8,128)}, f32[16,48,384]{2,1,0:T(8,128)}, f32[48,2304]...) custom-call(f32[48,128]{1,0:T(8,128)} %get-tuple-element.172.vsum, ...), custom_call_target="tpu_custom_call" | custom-call | tf_op jit(solution)/shard_map/pallas_call | solution.py:868
  248.8 18.3 %shard_map.310 = (bf16[384,384]{1,0:T(8,128)(2,1)}, bf16[1536,384]{1,0:T(8,128)(2,1)}) custom-call(s32[1]{0:T(128)} %bitcast.1.half, f32[384,384]{1,0:T(8,128)} %bitcast.97, f32[1536,384]{1,0:T(8,128)} %bitcast.87), custom_call_target="tpu_custom_call" | custom-call | tf_op jit(solution)/shard_map/pallas_call | solution.py:817
  267.1 27.2 %shard_map.311 = (bf16[12,48,384]{2,1,0:T(8,128)(2,1)}, bf16[4,192,384]{2,1,0:T(8,128)(2,1)}, bf16[2,24,4224]{2,1,0:T(8,128)(2,1)}, f32[48,384]{1,0:T(8,128)}) custom-call(bf16[8,48,384]{2,1,0:T(8,128)(2,1)} %bitcast.102, bf16[8,192,384]{2,1,0:T(8,128)(2,1)} %bitcast.93, bf16[24,4224]{1,0:T(8,128)(2,1)} %get-tuple-element.184.gy1, ...), custom_call_target="tpu_custom_call" | custom-call | tf_op jit(solution)/shard_map/pallas_call | solution.py:868
  295.0 11.4 %shard_map.312 = (f32[576,384]{1,0:T(8,128)}, f32[576,384]{1,0:T(8,128)}, bf16[576,384]{1,0:T(8,128)(2,1)}, f32[768,384]{1,0:T(8,128)}, f32[768,384]{1,0:T(8,128...) custom-call(s32[1]{0:T(128)S(6)} %copy.37.scal, ...), custom_call_target="tpu_custom_call" | custom-call | tf_op jit(solution)/shard_map/pallas_call | solution.py:2383
  (4 shorter events, 0.1 us)
Async XLA Ops:
  0.7 3.4 %copy-start = (s32[3]{0:T(128)S(1)}, s32[3]{0:T(128)}, u32[]{:S(2)}) copy-start(s32[3]{0:T(128)} %param.20) | copy-start | bytes 40

commit v3 on v2

--- a/solution.py
+++ b/solution.py
@@ -1109,6 +1109,13 @@
             for to in range(2):
                 pl.when(half == to)(functools.partial(row_copy, to, finish))
 
+    @pl.when(role == from_role)
+    def _():
+        crossing = [(count - 1, 1), (0, 0)]
+        rest = [(i, part) for i in range(count) for part in range(2)]
+        for i, part in crossing + [unit_ for unit_ in rest if unit_ not in crossing]:
+            copy(i, part).start()
+
     row_sends(False)
     if swap is not None:
         mine, both, msend, mrecv = swap
@@ -1126,9 +1133,6 @@
 
     @pl.when(role == from_role)
     def _():
-        for i in range(count):
-            for part in range(2):
-                copy(i, part).start()
         for i in range(count):
             for part in range(2):
                 copy(i, part).wait_send()

time: 309 us -> 310 us (level)
  no operation moved by 1% of the time
where the time goes in v3:
time: 310 us; the launch traced here: 307 us
  Pallas kernels  304 us (98%)
    pallas_call x8, Pallas kernels, comm_call(): pl.pallas_call(kernel, out_shape=out_shape, in_specs=[ANY] * len(args) if...  220 us
    pallas_call x7, Pallas kernels, local_call(): pl.pallas_call(kernel, out_shape=out_shape, in_specs=in_specs, out_specs=...  73.4 us
    pallas_call x1, Pallas kernels, body(): pl.pallas_call(functools.partial(update_kernel, rates, pieces), grid=(gri...  11.4 us

profile of v3, /device:TPU:27, one launch (start us, length us, event | category | flops | bytes accessed | tf_op | source)
XLA Modules:
  0.0 307.1 jit_solution(1321034860398804221)
XLA Ops:
  0.7 0.0 copy-start
  0.7 3.4 %shard_map.297 = (bf16[4,48,384]{2,1,0:T(8,128)(2,1)}, bf16[4,48,384]{2,1,0:T(8,128)(2,1)}, bf16[2,192,384]{2,1,0:T(8,128)(2,1)}, bf16[48,1152]{1,0:T(8,128)(2,1...) custom-call(s32[1]{0:T(128)} %bitcast.role, s32[1]{0:T(128)} %bitcast.1.half, ...), custom_call_target="tpu_custom_call" | custom-call | tf_op jit(solution)/shard_map/pallas_call | solution.py:817
  4.1 0.0 copy-done
  4.2 0.1 copy.34
  4.3 0.1 copy.35
  4.4 0.1 multiply_sine_fusion
  4.5 0.1 copy.36
  4.6 0.1 concatenate.3
  4.7 0.6 pad.4.pt
  5.3 37.2 %shard_map.298 = (bf16[4,8,48,384]{3,2,1,0:T(8,128)(2,1)}, bf16[4,8,48,384]{3,2,1,0:T(8,128)(2,1)}, bf16[2,8,192,384]{3,2,1,0:T(8,128)(2,1)}, bf16[8,48,1152]{2,...) custom-call(bf16[4,48,384]{2,1,0:T(8,128)(2,1)} %get-tuple-element.113.pa, ...), custom_call_target="tpu_custom_call" | custom-call | tf_op jit(solution)/shard_map/pallas_call | solution.py:868
  42.5 3.1 %shard_map.299 = (f32[128,384]{1,0:T(8,128)}, f32[64,384]{1,0:T(8,128)}, f32[64,384]{1,0:T(8,128)}, f32[8,1152]{1,0:T(8,128)}, bf16[2,384,192]{2,1,0:T(8,128)(2,1)}, /*index=5*/f32[8,128]{1,0:T(8,128)}) custom-call(s32[1]{0:T(128)} %bitcast.2.rank, f32[64,384]{1,0:T(8,128)} %bitcast.100, bf16[384,1152]{1,0:T(8,128)(2,1)} %bitcast.81, bf16[384,1152]{1,0:T(8,128)(2,1)} %bitcast.95), custom_call_target="tpu_custom_call" | custom-call | tf_op jit(solution)/shard_map/pallas_call | solution.py:817
  45.6 3.0 shard_map.300.mq
  48.6 13.2 %shard_map.301 = (bf16[3,2,64,384]{3,2,1,0:T(8,128)(2,1)}, f32[3,304,192]{2,1,0:T(8,128)}, bf16[3,304,192]{2,1,0:T(8,128)(2,1)}, bf16[384,128]{1,0:T(8,128)(2,1)...) custom-call(s32[1]{0:T(128)} %bitcast.role, ...), custom_call_target="tpu_custom_call" | custom-call | tf_op jit(solution)/shard_map/pallas_call | solution.py:817
  61.8 15.2 %shard_map.302 = (bf16[3,2,64,384]{3,2,1,0:T(8,128)(2,1)}, bf16[3,304,192]{2,1,0:T(8,128)(2,1)}, f32[2,8,1152]{2,1,0:T(8,128)}) custom-call(bf16[3,2,64,384]{3,2,1,0:T(8,128)(2,1)} %get-tuple-element.134.h1s, bf16[3,304,192]{2,1,0:T(8,128)(2,1)} %get-tuple-element.135.gq, f32[2,8,1152]{2,1,0:T(8,128)} %shard_map.300.mq), custom_call_target="tpu_custom_call" | custom-call | tf_op jit(solution)/shard_map/pallas_call | solution.py:868
  77.1 6.7 %shard_map.303 = (bf16[3,2,64,384]{3,2,1,0:T(8,128)(2,1)}, bf16[10,384,384]{2,1,0:T(8,128)(2,1)}, bf16[2,384,384]{2,1,0:T(8,128)(2,1)}, bf16[2,384,1536]{2,1,0:T...) custom-call(s32[1]{0:T(128)} %bitcast.role, ...), custom_call_target="tpu_custom_call" | custom-call | tf_op jit(solution)/shard_map/pallas_call | solution.py:817
  83.7 38.2 %shard_map.304 = (bf16[3,2,64,384]{3,2,1,0:T(8,128)(2,1)}, f32[2,304,384]{2,1,0:T(8,128)}) custom-call(bf16[3,2,64,384]{3,2,1,0:T(8,128)(2,1)} %get-tuple-element.141.dh1, f32[2,2,304,384]{3,2,1,0:T(8,128)} %get-tuple-element.142.dkv), custom_call_target="tpu_custom_call" | custom-call | tf_op jit(solution)/shard_map/pallas_call | solution.py:868
  122.0 16.4 %shard_map.305 = (bf16[6,384,384]{2,1,0:T(8,128)(2,1)}, bf16[2,384,384]{2,1,0:T(8,128)(2,1)}, bf16[2,384,1536]{2,1,0:T(8,128)(2,1)}, bf16[2,2,304,384]{3,2,1,0:T...) custom-call(s32[1]{0:T(128)} %bitcast.role, s32[1]{0:T(128)} %bitcast.1.half, ...), custom_call_target="tpu_custom_call" | custom-call | tf_op jit(solution)/shard_map/pallas_call | solution.py:817
  138.3 6.0 %shard_map.306 = (bf16[10,384,384]{2,1,0:T(8,128)(2,1)}, bf16[2,384,384]{2,1,0:T(8,128)(2,1)}, bf16[2,384,1536]{2,1,0:T(8,128)(2,1)}, bf16[2,304,384]{2,1,0:T(8,...) custom-call(bf16[6,384,384]{2,1,0:T(8,128)(2,1)} %get-tuple-element.147.acts_s, ...), custom_call_target="tpu_custom_call" | custom-call | tf_op jit(solution)/shard_map/pallas_call | solution.py:868
  144.3 12.3 %shard_map.307 = (f32[9,4,48,384]{3,2,1,0:T(8,128)}, bf16[9,4,48,384]{3,2,1,0:T(8,128)(2,1)}, bf16[4,2,24,4224]{3,2,1,0:T(8,128)(2,1)}) custom-call(s32[1]{0:T(128)} %bitcast.role, s32[1]{0:T(128)} %bitcast.1.half, s32[1]{0:T(128)} %bitcast.2.rank, bf16[6,384,384]{2,1,0:T(8,128)(2,1)} %get-tuple-element.147.acts_s, ...), custom_call_target="tpu_custom_call" | custom-call | tf_op jit(solution)/shard_map/pallas_call | solution.py:817
  156.7 71.0 %shard_map.308 = (f32[9,48,384]{2,1,0:T(8,128)}, bf16[24,4224]{1,0:T(8,128)(2,1)}, f32[48,128]{1,0:T(8,128)}, f32[8,384]{1,0:T(8,128)}, f32[48,2304]{1,0:T(8,128...) custom-call(f32[9,4,48,384]{3,2,1,0:T(8,128)} %get-tuple-element.164.own_in, bf16[9,4,48,384]{3,2,1,0:T(8,128)(2,1)} %get-tuple-element.165.snd, ...), custom_call_target="tpu_custom_call" | custom-call | tf_op jit(solution)/shard_map/pallas_call | solution.py:868
  227.7 21.9 %shard_map.309 = (f32[8,48,384]{2,1,0:T(8,128)}, f32[8,4,48,384]{3,2,1,0:T(8,128)}, f32[12,48,384]{2,1,0:T(8,128)}, f32[16,48,384]{2,1,0:T(8,128)}, f32[48,2304]...) custom-call(f32[48,128]{1,0:T(8,128)} %get-tuple-element.172.vsum, ...), custom_call_target="tpu_custom_call" | custom-call | tf_op jit(solution)/shard_map/pallas_call | solution.py:868
  249.6 18.3 %shard_map.310 = (bf16[384,384]{1,0:T(8,128)(2,1)}, bf16[1536,384]{1,0:T(8,128)(2,1)}) custom-call(s32[1]{0:T(128)} %bitcast.1.half, f32[384,384]{1,0:T(8,128)} %bitcast.97, f32[1536,384]{1,0:T(8,128)} %bitcast.87), custom_call_target="tpu_custom_call" | custom-call | tf_op jit(solution)/shard_map/pallas_call | solution.py:817
  268.0 26.9 %shard_map.311 = (bf16[12,48,384]{2,1,0:T(8,128)(2,1)}, bf16[4,192,384]{2,1,0:T(8,128)(2,1)}, bf16[2,24,4224]{2,1,0:T(8,128)(2,1)}, f32[48,384]{1,0:T(8,128)}) custom-call(bf16[8,48,384]{2,1,0:T(8,128)(2,1)} %bitcast.102, bf16[8,192,384]{2,1,0:T(8,128)(2,1)} %bitcast.93, bf16[24,4224]{1,0:T(8,128)(2,1)} %get-tuple-element.184.gy1, ...), custom_call_target="tpu_custom_call" | custom-call | tf_op jit(solution)/shard_map/pallas_call | solution.py:868
  295.5 11.4 %shard_map.312 = (f32[576,384]{1,0:T(8,128)}, f32[576,384]{1,0:T(8,128)}, bf16[576,384]{1,0:T(8,128)(2,1)}, f32[768,384]{1,0:T(8,128)}, f32[768,384]{1,0:T(8,128...) custom-call(s32[1]{0:T(128)S(6)} %copy.37.scal, ...), custom_call_target="tpu_custom_call" | custom-call | tf_op jit(solution)/shard_map/pallas_call | solution.py:2387
  (4 shorter events, 0.1 us)
Async XLA Ops:
  0.7 3.4 %copy-start = (s32[3]{0:T(128)S(1)}, s32[3]{0:T(128)}, u32[]{:S(2)}) copy-start(s32[3]{0:T(128)} %param.20) | copy-start | bytes 40
